TPU v7x, 256 devices: a whole 4x4x8 slice. The times are simulated.
256 devices in a mesh: box: 64 (over y, z, core), sib: 4 (over x).
Axes of the slice: x: 4, y: 4, z: 8, core: 2. Of those that a mesh axis runs over, the one named last changes fastest.
Arguments:
- self_blocks: float32 [64, 8, 512, 512], P('box', 'sib'), may hold values from -16 to 96, as said below
- orders: int32 [64, 8, 512], P('box', 'sib'), may hold values from 0 to 511, each once within a row
- interpolation: float32 [64, 8, 128, 384], P('box', 'sib'), may hold values from -0.5 to 0.5
- couplings: bfloat16 [64, 8, 512, 16, 128], P('box', 'sib'), may hold values from -0.19921875 to 0.19921875
- neighbours: int32 [64, 8, 16], P('box', 'sib'), may hold values from 0 to 511, as said below
Outputs:
- updated_couplings: bfloat16 [64, 8, 128, 16, 128], P('box', 'sib')
- parent_matrix: float32 [64, 1024, 1024], P('box', 'sib')
Inputs may be any that keep to these rules, and one draw needn't show every extreme that they name: `neighbours`: entries 0 to 3 of each list name distinct other children of the same parent. The other entries name children of other parents whose child number c2 has the same c2 // 2 as the box's own, and whose parent number is the box's own plus (j * 32) // 12 or minus (j * 31) // 12, for j from 1 to 12, counted around the end. For each of these 24 differences, exactly 1 far entries of the 2 boxes on one device name it when 2 * 12 is a multiple of 24, else 1 or 0, with 1 reached. Entries of one list may repeat. `self_blocks`: each block is symmetric positive definite.
All inputs are finite; a program needn't handle non-finite values.
Results may differ from a plain program's by a relative error of at most 0.001.
Values sent between devices are 32-bit elements; how exact they have to be, the bound alone decides.
No kernel may reach another device: no remote copies, remote signals or barrier semaphores. Data moves between devices by JAX's collectives and lax.ppermute only.
A program may use at most 128 MiB of HBM per device.

v0:
```python
import functools
import jax
import jax.numpy as jnp
import numpy as np
from jax import lax
from jax.experimental import pallas as pl
from jax.experimental.pallas import tpu as pltpu
from jax.sharding import PartitionSpec as P


NSIB = 4
HIGH = lax.Precision.HIGHEST
F32 = jnp.float32
BF16 = jnp.bfloat16
NT = (((1,), (1,)), ((), ()))
NN = (((1,), (0,)), ((), ()))


def dot_high(a, b, dims=NN):
    return lax.dot_general(a, b, dims, precision=HIGH, preferred_element_type=F32)


def dot_bf16(a, b, dims=NN):
    return lax.dot_general(a, b, dims, preferred_element_type=F32)


def split2(x):
    hi = x.astype(BF16)
    return hi, (x - hi.astype(F32)).astype(BF16)


def split3(x):
    hi = x.astype(BF16)
    rest = x - hi.astype(F32)
    mid = rest.astype(BF16)
    return hi, mid, (rest - mid.astype(F32)).astype(BF16)


def iota(shape, dim):
    return lax.broadcasted_iota(jnp.int32, shape, dim)


def spread(x, lane):
    return jnp.take_along_axis(x, jnp.full(x.shape, lane, jnp.int32), axis=1)


def eliminate_rows(panels, base):
    shape = panels[0].shape
    lane, sub = iota(shape, 1), iota(shape, 0)
    panels = list(panels)
    columns = [[spread(panel, base + t) for t in range(8)] for panel in panels]
    inverses = [jnp.ones(shape, F32) for _ in panels]
    for t in range(8):
        here = lane == base + t
        one = (sub == t).astype(F32)
        for b, panel in enumerate(panels):
            column = columns[b][t]
            inverse = 1.0 / jnp.broadcast_to(column[t : t + 1, :], shape)
            inverses[b] = jnp.where(sub == t, inverse, inverses[b])
            ratio = jnp.where(sub > t, column, 0.0) * inverse
            for u in range(t + 1, 8):
                later = columns[b][u]
                columns[b][u] = later - ratio * jnp.broadcast_to(later[t : t + 1, :], shape)
            row = jnp.where(here, 1.0, jnp.broadcast_to(panel[t : t + 1, :], shape))
            panels[b] = jnp.where(here, one, panel) - ratio * row
    return panels, inverses


def invert_cholesky(blocks):
    count, size, span = len(blocks), blocks[0].shape[0], 32
    lane, sub = iota((8, size), 1), iota((8, size), 0)
    rows = [[block[8 * g : 8 * g + 8, :] for g in range(size // 8)] for block in blocks]
    out = [[] for _ in blocks]
    for start in range(0, size, span):
        end = start + span
        finals, scaled_rows = [[] for _ in blocks], [[] for _ in blocks]
        for g in range(start // 8, end // 8):
            base = 8 * g
            panels, inverses = eliminate_rows([rows[b][g] for b in range(count)], base)
            for b in range(count):
                panel = panels[b]
                scaled = panel * inverses[b]
                beyond = lane > sub + base
                out[b].append(jnp.where(beyond, 0.0, panel * jnp.sqrt(inverses[b])))
                finals[b].append(panel)
                scaled_rows[b].append(jnp.where(beyond & (lane < end), 0.0, scaled))
                if base + 8 == end:
                    continue
                scaled = jnp.where(beyond & (lane < base + 8), 0.0, scaled)
                flipped = panel.T
                clear = (lane >= base) & (lane < base + 8)
                for i in range(g + 1, end // 8):
                    factors = flipped[8 * i : 8 * i + 8, :]
                    terms = [
                        jnp.broadcast_to(factors[:, t : t + 1], (8, size))
                        * jnp.broadcast_to(scaled[t : t + 1, :], (8, size))
                        for t in range(8)
                    ]
                    while len(terms) > 1:
                        terms = [terms[j] + terms[j + 1] for j in range(0, len(terms), 2)]
                    rows[b][i] = jnp.where(clear, 0.0, rows[b][i]) - terms[0]
        if end < size:
            clear = (lane >= start) & (lane < end)
            for b in range(count):
                factors = jnp.concatenate(finals[b], axis=0).T[end:]
                update = dot_high(factors, jnp.concatenate(scaled_rows[b], axis=0))
                for i in range(end // 8, size // 8):
                    k = 8 * i - end
                    rows[b][i] = jnp.where(clear, 0.0, rows[b][i]) - update[k : k + 8]
    return [jnp.concatenate(parts, axis=0) for parts in out]


def factor_kernel(blocks_ref, orders_ref, interp_ref, high_ref, low_ref, own_ref, work, aug):
    count, dof, _ = blocks_ref.shape
    skel, red = interp_ref.shape[1:]
    for b in range(count):
        order = orders_ref[b : b + 1, :]
        place_t = (iota((dof, dof), 0) == order).astype(F32).astype(BF16)
        column = jnp.broadcast_to(order.astype(F32), (128, dof)).T
        lanes = iota((dof, 128), 1).astype(F32)
        place = jnp.concatenate(
            [(column == lanes + 128.0 * q).astype(F32) for q in range(dof // 128)], axis=1
        )
        place_b = place.astype(BF16)
        parts = [dot_bf16(place_b, part).astype(BF16) for part in split3(blocks_ref[b])]
        ordered = dot_bf16(parts[0], place_t) + (
            dot_bf16(parts[1], place_t) + dot_bf16(parts[2], place_t)
        )
        a_ss = ordered[:skel, :skel]
        a_sr = ordered[:skel, skel:]
        interp = interp_ref[b]
        interp_t = interp.T
        bar_sr = a_sr - dot_high(a_ss, interp)
        left = jnp.concatenate([a_sr.T, interp_t], axis=1)
        right = jnp.concatenate([interp, bar_sr], axis=0)
        work[b] = ordered[skel:, skel:] - dot_high(left, right)
        pieces = [dot_bf16(part, place_b[:skel]) for part in split3(interp_t)]
        aug[b, :, :dof] = place[skel:] - (pieces[0] + (pieces[1] + pieces[2]))
        aug[b, :, dof:] = bar_sr.T
        own_ref[b] = a_ss
    panels = red // 128
    for k in range(panels):
        lo, hi = 128 * k, 128 * (k + 1)
        inverses = invert_cholesky([work[b, lo:hi, lo:hi] for b in range(count)])
        for b in range(count):
            solved = dot_high(inverses[b], aug[b, lo:hi, :])
            aug[b, lo:hi, :] = solved
            if hi < red:
                panel = dot_high(work[b, hi:, lo:hi], inverses[b], NT)
                work[b, hi:, hi:] = work[b, hi:, hi:] - dot_high(panel, panel, NT)
                aug[b, hi:, :] = aug[b, hi:, :] - dot_high(panel, solved)
    for b in range(count):
        solved_t = aug[b, :, dof:].T
        own_ref[b] = own_ref[b] - dot_high(solved_t, aug[b, :, dof:])
        grid_high, grid_low = split2(aug[b, :, :dof])
        high_ref[b, :red] = grid_high
        low_ref[b, :red] = grid_low
        column = jnp.broadcast_to(orders_ref[b : b + 1, :].astype(F32), (128, dof)).T
        lanes = iota((skel, 128), 1).astype(F32)
        place_s = jnp.concatenate(
            [(column[:skel] == lanes + 128.0 * q).astype(F32) for q in range(dof // 128)], axis=1
        )
        last_high, last_low = split2(place_s - dot_high(solved_t, aug[b, :, :dof]))
        high_ref[b, red:] = last_high
        low_ref[b, red:] = last_low


def factor(self_blocks, orders, interpolation, interpret=False):
    count, dof, _ = self_blocks.shape
    skel, red = interpolation.shape[1:]
    return pl.pallas_call(
        factor_kernel,
        out_shape=(
            jax.ShapeDtypeStruct((count, dof, dof), BF16),
            jax.ShapeDtypeStruct((count, dof, dof), BF16),
            jax.ShapeDtypeStruct((count, skel, skel), F32),
        ),
        scratch_shapes=[pltpu.VMEM((count, red, red), F32), pltpu.VMEM((count, red, dof + skel), F32)],
        compiler_params=pltpu.CompilerParams(vmem_limit_bytes=24 << 20),
        cost_estimate=pl.CostEstimate(flops=8 << 30, bytes_accessed=6 << 20, transcendentals=0),
        interpret=interpret,
        name="factor",
    )(self_blocks, orders, interpolation)


def pack_symmetric(block, flag):
    half = block.shape[0] // 2
    top, bottom = block[:half], block[half:]
    lane, row = iota((half, 128), 1), iota((half, 128), 0)
    turned = pltpu.roll(bottom, half, 1)
    body = jnp.where((lane >= half) | (lane > row), top, turned)
    diagonal = jnp.sum(jnp.where(lane == row, top, 0.0), axis=0, keepdims=True)
    return body, jnp.where(iota((1, 128), 1) < half, diagonal, flag)


def unpack_symmetric(body, tail):
    half = 64
    lane, row = iota((half, 128), 1), iota((half, 128), 0)
    upper = jnp.where((lane >= half) | (lane > row), body, 0.0)
    inner = jnp.where(lane < half, body, 0.0)
    lower = pltpu.roll(jnp.where(lane < row, inner, 0.0), half, 1)
    strict = jnp.concatenate([upper, lower], axis=0)
    first = jnp.where(lane == row, jnp.broadcast_to(tail, (half, 128)), 0.0)
    second = pltpu.roll(jnp.where(lane == row, inner, 0.0), half, 1)
    return strict + strict.T + jnp.concatenate([first, second], axis=0)


Y, Z, C = 4, 8, 2
STAGES = [(dy, dc) for dy in range(Y) for dc in range(C)]
TABLE = 128


def place_of(box):
    return box // (Z * C), box // C % Z, box % C


def box_of(y, z, c):
    return (y % Y * Z + z % Z) * C + c % C


def plan(boxes, reach):
    steps = [(j * (boxes // 2)) // reach for j in range(1, reach + 1)]
    steps += [boxes - (j * ((boxes - 1) // 2)) // reach for j in range(1, reach + 1)]
    lists = []
    for box in range(boxes):
        y, z, c = place_of(box)
        by_stage = {stage: [] for stage in STAGES}
        for step in steps:
            ty, tz, tc = place_of((box + step) % boxes)
            by_stage[(ty - y) % Y, (tc - c) % C].append((step, (tz - z) % Z))
        lists.append(by_stage)
    caps = [max(len(found[stage]) for found in lists) for stage in STAGES]
    starts = np.concatenate([[0], np.cumsum(caps)]).tolist()
    table = np.zeros((boxes, TABLE), np.int32)
    for box in range(boxes):
        y, z, c = place_of(box)
        for s, stage in enumerate(STAGES):
            for j, (step, _) in enumerate(lists[box][stage]):
                table[box, step] = starts[s] + j
            source = lists[box_of(y - stage[0], z, c - stage[1])]
            for j, (_, shift) in enumerate(source[stage]):
                table[box, boxes + starts[s] + j] = shift
    return table, caps, starts


def row_spec(table):
    return pl.BlockSpec(
        (8, table.shape[1]), lambda *args: (args[-1][0] // 8, 0), memory_space=pltpu.SMEM
    )


def gram(z_t):
    high, low = split2(z_t)
    return dot_bf16(high, high, NT) + (dot_bf16(high, low, NT) + dot_bf16(low, high, NT))


def slot_updates(high_ref, low_ref, slot_pair):
    product = dot_bf16(high_ref[0], slot_pair) + dot_bf16(low_ref[0], slot_pair)
    both = gram(product.T)
    return both[:128, :128], both[128:, 128:]


def far_kernel(ids_ref, where_ref, table_ref, high_ref, low_ref, w_ref, *rest, caps, starts, boxes):
    outs, (bodies, tails) = rest[: len(caps)], rest[len(caps) :]
    box = pl.program_id(0)
    parent = where_ref[0]

    @pl.when(box == 0)
    def _():
        bodies[...] = jnp.zeros_like(bodies)
        tails[...] = jnp.zeros_like(tails)

    slots = w_ref.shape[2]
    by_slot = jnp.swapaxes(w_ref[0], 0, 1)
    for first in range(NSIB, slots, 2):
        pair = jnp.concatenate([by_slot[first], by_slot[first + 1]], axis=1)
        for s, update in enumerate(slot_updates(high_ref, low_ref, pair)):
            other = ids_ref[box, first + s]
            body, tail = pack_symmetric(update, (other & 1).astype(F32))
            place = table_ref[parent & 7, ((other >> 3) - parent) & (boxes - 1)]
            bodies[place] = body
            tails[pl.ds(place, 1), :] = tail

    @pl.when(box == pl.num_programs(0) - 1)
    def _():
        for s, out in enumerate(outs):
            for j in range(caps[s]):
                out[64 * j : 64 * j + 64] = bodies[starts[s] + j]
            out[64 * caps[s] : 64 * caps[s] + 8] = jnp.concatenate(
                [tails[starts[s] : starts[s] + caps[s]], jnp.zeros((8 - caps[s], 128), F32)], axis=0
            )


def far_updates(ids, where, table, high, low, w, caps, starts, boxes, interpret=False):
    count, dof, slots, skel = w.shape
    red = dof - skel
    whole = lambda shape: pl.BlockSpec(shape, lambda b, *_: (0,) * len(shape))
    by_box = lambda shape: pl.BlockSpec((1,) + shape, lambda b, *_: (b,) + (0,) * len(shape))
    outs = [(64 * cap + 8, 128) for cap in caps]
    return pl.pallas_call(
        functools.partial(far_kernel, caps=caps, starts=starts, boxes=boxes),
        out_shape=[jax.ShapeDtypeStruct(shape, F32) for shape in outs],
        grid_spec=pltpu.PrefetchScalarGridSpec(
            num_scalar_prefetch=2,
            grid=(count,),
            in_specs=[row_spec(table)]
            + [by_box((red, dof)), by_box((red, dof)), by_box((dof, slots, skel))],
            out_specs=[whole(shape) for shape in outs],
            scratch_shapes=[
                pltpu.VMEM((starts[-1], 64, 128), F32),
                pltpu.VMEM((-(-starts[-1] // 8) * 8, 128), F32),
            ],
        ),
        compiler_params=pltpu.CompilerParams(vmem_limit_bytes=28 << 20),
        cost_estimate=pl.CostEstimate(flops=6 << 30, bytes_accessed=8 << 20, transcendentals=0),
        interpret=interpret,
        name="far_updates",
    )(ids, where, table, high, low, w)


def near_kernel(ids_ref, where_ref, high_ref, low_ref, last_high_ref, last_low_ref, w_ref, *rest):
    updated_ref, sib_outs, sib = rest[0], rest[1:-1], rest[-1]
    box = pl.program_id(0)
    this_sib = where_ref[1]

    @pl.when(box == 0)
    def _():
        sib[...] = jnp.zeros_like(sib)

    slots = w_ref.shape[2]
    by_slot = jnp.swapaxes(w_ref[0], 0, 1)
    coupled_slots = []
    for first in range(0, slots, 2):
        pair = jnp.concatenate([by_slot[first], by_slot[first + 1]], axis=1)
        coupled = dot_bf16(last_high_ref[0], pair) + dot_bf16(last_low_ref[0], pair)
        coupled_slots += [coupled[:, :128].astype(BF16), coupled[:, 128:].astype(BF16)]
        if first >= NSIB:
            continue
        for s, update in enumerate(slot_updates(high_ref, low_ref, pair)):
            other = ids_ref[box, first + s]
            child = other & 1
            body, tail = pack_symmetric(update, child.astype(F32))
            place = ((((other >> 1) & 3) - this_sib) & 3) * 2 + child
            rows = pl.ds(pl.multiple_of(box * 128, 128), 128)
            sib[place, rows, :] = coupled[:, 128 * s : 128 * s + 128]
            sib[place, 256:320, :] = sib[place, 256:320, :] + body
            sib[place, 320:321, :] = sib[place, 320:321, :] + tail
    updated_ref[0] = jnp.swapaxes(jnp.stack(coupled_slots), 0, 1)

    @pl.when(box == pl.num_programs(0) - 1)
    def _():
        for i, out in enumerate(sib_outs):
            out[...] = sib[2 * i : 2 * i + 2]


def near_updates(ids, where, high, low, w, interpret=False):
    count, dof, slots, skel = w.shape
    red = dof - skel
    by_box = lambda shape: pl.BlockSpec((1,) + shape, lambda b, *_: (b,) + (0,) * len(shape))
    last = pl.BlockSpec((1, skel, dof), lambda b, *_: (b, red // skel, 0))
    return pl.pallas_call(
        near_kernel,
        out_shape=(
            [jax.ShapeDtypeStruct((count, skel, slots, skel), BF16)]
            + [jax.ShapeDtypeStruct((2, 328, 128), F32)] * 4
        ),
        grid_spec=pltpu.PrefetchScalarGridSpec(
            num_scalar_prefetch=2,
            grid=(count,),
            in_specs=[
                by_box((red, dof)),
                by_box((red, dof)),
                last,
                last,
                by_box((dof, slots, skel)),
            ],
            out_specs=[by_box((skel, slots, skel))]
            + [pl.BlockSpec((2, 328, 128), lambda b, *_: (0, 0, 0))] * 4,
            scratch_shapes=[pltpu.VMEM((8, 328, 128), F32)],
        ),
        compiler_params=pltpu.CompilerParams(vmem_limit_bytes=28 << 20),
        cost_estimate=pl.CostEstimate(flops=3 << 30, bytes_accessed=8 << 20, transcendentals=0),
        interpret=interpret,
        name="near_updates",
    )(ids, where, high, low, high, low, w)


def route_kernel(where_ref, table_ref, *rest, caps, starts, boxes):
    got, outs, sums = rest[: len(caps)], rest[len(caps) : -1], rest[-1]
    row = where_ref[0] & 7
    sums[...] = jnp.zeros_like(sums)
    for s, block in enumerate(got):
        for j in range(caps[s]):
            shift = table_ref[row, boxes + starts[s] + j]
            body = block[64 * j : 64 * j + 64]
            tail = block[64 * caps[s] + j : 64 * caps[s] + j + 1]
            second = tail[:, 64:65]
            share = jnp.broadcast_to(second, body.shape)
            row_share = jnp.broadcast_to(second, tail.shape)
            sums[shift, 0:64] = sums[shift, 0:64] + body * (1.0 - share)
            sums[shift, 64:128] = sums[shift, 64:128] + body * share
            sums[shift, 128:129] = sums[shift, 128:129] + tail * (1.0 - row_share)
            sums[shift, 129:130] = sums[shift, 129:130] + tail * row_share
    for out, shifts in zip(outs, ROUTES):
        for i, shift in enumerate(shifts):
            out[PAIR * i : PAIR * (i + 1)] = sums[shift]


PAIR = 136
ROUTES = ((0,), (1, 3), (7, 5), (4,), (2,), (6,))


def route(where, table, got, caps, starts, boxes, interpret=False):
    whole = lambda shape: pl.BlockSpec(shape, lambda b, *_: (0,) * len(shape))
    outs = [(PAIR * len(shifts), 128) for shifts in ROUTES]
    return pl.pallas_call(
        functools.partial(route_kernel, caps=caps, starts=starts, boxes=boxes),
        out_shape=[jax.ShapeDtypeStruct(shape, F32) for shape in outs],
        grid_spec=pltpu.PrefetchScalarGridSpec(
            num_scalar_prefetch=1,
            grid=(1,),
            in_specs=[row_spec(table)] + [whole(block.shape) for block in got],
            out_specs=[whole(shape) for shape in outs],
            scratch_shapes=[pltpu.VMEM((Z, PAIR, 128), F32)],
        ),
        compiler_params=pltpu.CompilerParams(vmem_limit_bytes=16 << 20),
        cost_estimate=pl.CostEstimate(flops=1 << 22, bytes_accessed=2 << 20, transcendentals=0),
        interpret=interpret,
        name="route",
    )(where, table, *got)


def fold_kernel(up_ref, down_ref, two_ref, six_ref, out_two, out_six):
    out_two[...] = two_ref[...] + up_ref[PAIR:]
    out_six[...] = six_ref[...] + down_ref[PAIR:]


def fold(up, down, two, six, interpret=False):
    vmem = pl.BlockSpec(memory_space=pltpu.VMEM)
    return pl.pallas_call(
        fold_kernel,
        out_shape=[jax.ShapeDtypeStruct((PAIR, 128), F32)] * 2,
        in_specs=[vmem] * 4,
        out_specs=[vmem] * 2,
        compiler_params=pltpu.CompilerParams(vmem_limit_bytes=4 << 20),
        cost_estimate=pl.CostEstimate(flops=1 << 17, bytes_accessed=1 << 18, transcendentals=0),
        interpret=interpret,
        name="fold",
    )(up, down, two, six)


def assemble_kernel(where_ref, own_ref, *rest):
    far = rest[:-8]
    kept = rest[-8:-4]
    got = rest[-4:-1]
    out_ref = rest[-1]
    sibs = [kept[0]] + list(got)
    skeleton = []
    for c in range(2):
        body = sum(block[64 * c : 64 * c + 64] for block in far)
        tail = sum(block[128 + c : 129 + c] for block in far)
        for other in sibs:
            body = body + other[c, 256:320, :]
            tail = tail + other[c, 320:321, :]
        skeleton.append(own_ref[c] - unpack_symmetric(body, tail))
    here = where_ref[1]
    wide = lambda ref: jnp.concatenate([ref[0, 0:256, :], ref[1, 0:256, :]], axis=1)
    zero = jnp.zeros((128, 128), F32)
    first = wide(kept[0]) + jnp.concatenate(
        [
            jnp.concatenate([skeleton[0], zero], axis=1),
            jnp.concatenate([zero, skeleton[1]], axis=1),
        ],
        axis=0,
    )
    out_ref[:, pl.ds(pl.multiple_of(here * 256, 256), 256)] = 0.5 * (first + first.T)
    for s in range(1, 4):
        column = (here + 4 - s) & 3
        block = 0.5 * (wide(kept[4 - s]) + wide(got[s - 1]).T)
        out_ref[:, pl.ds(pl.multiple_of(column * 256, 256), 256)] = block


def assemble(where, own, far, kept, got, interpret=False):
    vmem = pl.BlockSpec(memory_space=pltpu.VMEM)
    args = [own, *far, *kept, *got]
    return pl.pallas_call(
        assemble_kernel,
        out_shape=jax.ShapeDtypeStruct((256, 1024), F32),
        in_specs=[pl.BlockSpec(memory_space=pltpu.SMEM)] + [vmem] * len(args),
        out_specs=vmem,
        compiler_params=pltpu.CompilerParams(vmem_limit_bytes=24 << 20),
        interpret=interpret,
        name="assemble",
    )(where, *args)


def on_device(self_blocks, orders, interpolation, couplings, neighbours):
    boxes = lax.axis_size("box")
    sibs = lax.axis_size("sib")
    parent, sib = lax.axis_index("box"), lax.axis_index("sib")
    count = orders.shape[1]
    slots = couplings.shape[3]
    where = jnp.stack([parent, sib]).astype(jnp.int32)
    plans, caps, starts = plan(boxes, (slots - NSIB) * count // 2)
    table = jnp.asarray(plans)
    high, low, own = factor(self_blocks[0], orders[0], interpolation[0])
    ids = neighbours[0]
    sent = far_updates(ids, where, table, high, low, couplings[0], caps, starts, boxes)

    def shifted(block, dy, dz, dc):
        moves = []
        for i in range(boxes):
            y, z, c = place_of(i)
            moves.append((i, box_of(y + dy, z + dz, c + dc)))
        return lax.ppermute(block, "box", moves)

    got = [sent[0]]
    for (dy, dc), block in zip(STAGES[1:], sent[1:]):
        got.append(shifted(block, dy, 0, dc))
    updated, *kept = near_updates(ids, where, high, low, couplings[0])
    sib_got = [
        lax.ppermute(kept[s], "sib", [(i, (i + s) % sibs) for i in range(sibs)])
        for s in range(1, sibs)
    ]
    here, up, down, four, two, six = route(where, table, got, caps, starts, boxes)
    up = shifted(up, 0, 1, 0)
    down = shifted(down, 0, -1, 0)
    four = shifted(four, 0, 4, 0)
    two, six = fold(up, down, two, six)
    far = [here, up, down, four, shifted(two, 0, 2, 0), shifted(six, 0, -2, 0)]
    rows = assemble(where, own, far, kept, sib_got)
    return updated[None], rows[None]


def solution(mesh):
    return jax.shard_map(
        on_device,
        mesh=mesh,
        in_specs=(
            P("box", "sib", None, None),
            P("box", "sib", None),
            P("box", "sib", None, None),
            P("box", "sib", None, None, None),
            P("box", "sib", None),
        ),
        out_specs=(P("box", "sib", None, None, None), P("box", "sib", None)),
        check_vma=False,
    )
```

profile of v0, /device:TPU:2, one launch (start us, length us, event | category | flops | bytes accessed | tf_op | source)
XLA Modules:
  0.0 89.7 jit_solution(14720786776562986235)
XLA Ops:
  0.6 0.1 pad_add_fusion.where_ref
  0.7 1.6 %copy-done.2 = f32[1,2,512,512]{3,2,1,0:T(8,128)S(1)} copy-done((f32[1,2,512,512]{3,2,1,0:T(8,128)S(1)}, f32[1,2,512,512]{3,2,1,0:T(8,128)}, u32[]{:S(2)}) %copy-start.2) | copy-done | bytes 2097176
  2.3 1.0 %copy-done.3 = f32[1,2,128,384]{3,2,1,0:T(8,128)S(1)} copy-done((f32[1,2,128,384]{3,2,1,0:T(8,128)S(1)}, f32[1,2,128,384]{3,2,1,0:T(8,128)}, u32[]{:S(2)}) %copy-start.3) | copy-done | bytes 393240
  3.3 0.7 copy-done.4
  4.0 28.8 %factor.1 = (bf16[2,512,512]{2,1,0:T(8,128)(2,1)S(1)}, bf16[2,512,512]{2,1,0:T(8,128)(2,1)S(1)}, f32[2,128,128]{2,1,0:T(8,128)S(1)}) custom-call(f32[2,512,512]{2,1,0:T(8,128)S(1)} %bitcast.11, s32[2,512]{1,0:T(2,128)S(1)} %bitcast.13, f32[2,128,384]{2,1,0:T(8,128)S(1)} %bitcast.12), custom_call_target="tpu_custom_call" | custom-call | flops 8589934592 | bytes 6291456 | tf_op jit(solution)/shard_map/factor/pallas_call | solution.py:171
  32.8 8.0 %far_updates.1 = (f32[264,128]{1,0:T(8,128)S(1)}, f32[200,128]{1,0:T(8,128)S(1)}, f32[264,128]{1,0:T(8,128)S(1)}, f32[136,128]{1,0:T(8,128)S(1)}, f32[264,128]{1...) custom-call(s32[2,16]{1,0:T(2,128)S(1)} %bitcast.14, ...), custom_call_target="tpu_custom_call" | custom-call | flops 6442450944 | bytes 8388608 | tf_op jit(solution)/shard_map/far_updates/pallas_call | solution.py:300
  40.9 0.1 collective-permute-start
  41.0 1.7 %collective-permute-start.2 = (f32[136,128]{1,0:T(8,128)S(1)}, f32[136,128]{1,0:T(8,128)S(1)}, u32[]{:S(2)}, u32[]{:S(2)}) collective-permute-start(f32[136,128]{1,0:T(8,128)S(1)} %get-tuple-element.33), channel_id=1, source_target_pairs={{0,68},{4,64},{8,76},{12,72},{16,84},{20,80},{24,92},{28,88},{32,1... | collective-permute-start | bytes 208904 | tf_op jit(solution)/shard_map/ppermute | solution.py:515
  42.6 1.4 %collective-permute-start.6 = (f32[200,128]{1,0:T(8,128)S(1)}, f32[200,128]{1,0:T(8,128)S(1)}, u32[]{:S(2)}, u32[]{:S(2)}) collective-permute-start(f32[200,128]{1,0:T(8,128)S(1)} %get-tuple-element.37), channel_id=1, source_target_pairs={{0,196},{4,192},{8,204},{12,200},{16,212},{20,208},{24,220},{28,21... | collective-permute-start | bytes 307208 | tf_op jit(solution)/shard_map/ppermute | solution.py:515
  44.1 0.3 collective-permute-start.1
  44.4 2.9 %collective-permute-start.3 = (f32[264,128]{1,0:T(8,128)S(1)}, f32[264,128]{1,0:T(8,128)S(1)}, u32[]{:S(2)}, u32[]{:S(2)}) collective-permute-start(f32[264,128]{1,0:T(8,128)S(1)} %get-tuple-element.34), channel_id=1, source_target_pairs={{0,128},{4,132},{8,136},{12,140},{16,144},{20,148},{24,152},{28,15... | collective-permute-start | bytes 405512 | tf_op jit(solution)/shard_map/ppermute | solution.py:515
  47.3 0.0 collective-permute-done.2.rest_3_
  47.3 1.2 %collective-permute-start.4 = (f32[264,128]{1,0:T(8,128)S(1)}, f32[264,128]{1,0:T(8,128)S(1)}, u32[]{:S(2)}, u32[]{:S(2)}) collective-permute-start(f32[264,128]{1,0:T(8,128)S(1)} %get-tuple-element.35), channel_id=1, source_target_pairs={{0,132},{4,128},{8,140},{12,136},{16,148},{20,144},{24,156},{28,15... | collective-permute-start | bytes 405512 | tf_op jit(solution)/shard_map/ppermute | solution.py:515
  48.4 1.8 %collective-permute-start.5 = (f32[264,128]{1,0:T(8,128)S(1)}, f32[264,128]{1,0:T(8,128)S(1)}, u32[]{:S(2)}, u32[]{:S(2)}) collective-permute-start(f32[264,128]{1,0:T(8,128)S(1)} %get-tuple-element.36), channel_id=1, source_target_pairs={{0,192},{4,196},{8,200},{12,204},{16,208},{20,212},{24,216},{28,22... | collective-permute-start | bytes 405512 | tf_op jit(solution)/shard_map/ppermute | solution.py:515
  50.2 6.3 %near_updates.1 = (bf16[2,128,16,128]{3,2,1,0:T(8,128)(2,1)}, f32[2,328,128]{2,1,0:T(8,128)S(1)}, f32[2,328,128]{2,1,0:T(8,128)S(1)}, f32[2,328,128]{2,1,0:T(8,128)S(1)}, f32[2,328,128]{2,1,0:T(8,128)S(1)}) custom-call(s32[2,16]{1,0:T(2,128)S(1)} %bitcast.15, s32[2]{0:T(128)S(1)} %pad_add_fusion.where_ref, ...), custom_call_target="tpu_custom_call" | custom-call | flops 3221225472 | bytes 8388608 | tf_op jit(solution)/shard_map/near_updates/pallas_call | solution.py:361
  56.5 0.0 collective-permute-done.6.rest_7_
  56.5 1.5 %collective-permute-start.12 = (f32[2,328,128]{2,1,0:T(8,128)S(1)}, f32[2,328,128]{2,1,0:T(8,128)S(1)}, u32[]{:S(2)}, u32[]{:S(2)}) collective-permute-start(f32[2,328,128]{2,1,0:T(8,128)S(1)} %get-tuple-element.47.rest_7_), channel_id=1, source_target_pairs={{0,1},{1,2},{2,3},{3,0},{4,5},{5,6},{6,7},{7,4},{8,9},{9,10},{10,1... | collective-permute-start | bytes 1007624 | tf_op jit(solution)/shard_map/ppermute | solution.py:522
  58.0 0.0 collective-permute-done.1.rest_2_
  58.0 2.8 %collective-permute-start.13 = (f32[2,328,128]{2,1,0:T(8,128)S(1)}, f32[2,328,128]{2,1,0:T(8,128)S(1)}, u32[]{:S(2)}, u32[]{:S(2)}) collective-permute-start(f32[2,328,128]{2,1,0:T(8,128)S(1)} %get-tuple-element.48.rest_8_), channel_id=1, source_target_pairs={{0,2},{1,3},{2,0},{3,1},{4,6},{5,7},{6,4},{7,5},{8,10},{9,11},{10,... | collective-permute-start | bytes 1007624 | tf_op jit(solution)/shard_map/ppermute | solution.py:522
  60.9 0.4 collective-permute-start.14
  61.3 0.0 collective-permute-done.4.rest_5_
  61.3 0.0 collective-permute-done.5.rest_6_
  61.3 1.5 %route.1 = (f32[136,128]{1,0:T(8,128)S(1)}, f32[272,128]{1,0:T(8,128)S(1)}, f32[272,128]{1,0:T(8,128)S(1)}, f32[136,128]{1,0:T(8,128)S(1)}, f32[136,128]{1,0:T(8,128)S(1)}, /*index=5*/f32[136,128]{1,0:T(8,128)S(1)}) custom-call(s32[2]{0:T(128)S(1)} %pad_add_fusion.where_ref, s32[64,128]{1,0:T(8,128)S(1)} %copy-done, ...), custom_call_target="tpu_custom_call" | custom-call | flops 4194304 | bytes 2097152 | tf_op jit(solution)/shard_map/route/pallas_call | solution.py:416
  62.8 2.0 %collective-permute-start.7 = (f32[272,128]{1,0:T(8,128)S(1)}, f32[272,128]{1,0:T(8,128)S(1)}, u32[]{:S(2)}, u32[]{:S(2)}) collective-permute-start(f32[272,128]{1,0:T(8,128)S(1)} %get-tuple-element.39), channel_id=1, source_target_pairs={{0,8},{4,12},{8,16},{12,20},{16,24},{20,28},{24,32},{28,36},{32,40... | collective-permute-start | bytes 417800 | tf_op jit(solution)/shard_map/ppermute | solution.py:515
  64.8 4.0 %collective-permute-start.8 = (f32[272,128]{1,0:T(8,128)S(1)}, f32[272,128]{1,0:T(8,128)S(1)}, u32[]{:S(2)}, u32[]{:S(2)}) collective-permute-start(f32[272,128]{1,0:T(8,128)S(1)} %get-tuple-element.40), channel_id=1, source_target_pairs={{0,56},{4,60},{8,0},{12,4},{16,8},{20,12},{24,16},{28,20},{32,24},... | collective-permute-start | bytes 417800 | tf_op jit(solution)/shard_map/ppermute | solution.py:515
  68.9 3.4 %collective-permute-done.7.up_ref.rest_1_ = f32[272,128]{1,0:T(8,128)S(1)} collective-permute-done((f32[272,128]{1,0:T(8,128)S(1)}, f32[272,128]{1,0:T(8,128)S(1)}, u32[]{:S(2)}, u32[]{:S(2)}) %collective-permute-start.7) | collective-permute-done | bytes 139296 | tf_op jit(solution)/shard_map/ppermute | solution.py:515
  72.2 4.3 %collective-permute-start.9 = (f32[136,128]{1,0:T(8,128)S(1)}, f32[136,128]{1,0:T(8,128)S(1)}, u32[]{:S(2)}, u32[]{:S(2)}) collective-permute-start(f32[136,128]{1,0:T(8,128)S(1)} %get-tuple-element.41), channel_id=1, source_target_pairs={{0,32},{4,36},{8,40},{12,44},{16,48},{20,52},{24,56},{28,60},{32,0... | collective-permute-start | bytes 208904 | tf_op jit(solution)/shard_map/ppermute | solution.py:515
  76.5 0.3 collective-permute-start.10
  76.9 4.8 %collective-permute-done.9.rest_3_ = f32[136,128]{1,0:T(8,128)S(1)} collective-permute-done((f32[136,128]{1,0:T(8,128)S(1)}, f32[136,128]{1,0:T(8,128)S(1)}, u32[]{:S(2)}, u32[]{:S(2)}) %collective-permute-start.9) | collective-permute-done | bytes 69664 | tf_op jit(solution)/shard_map/ppermute | solution.py:515
  81.7 4.0 %collective-permute-start.11 = (f32[136,128]{1,0:T(8,128)S(1)}, f32[136,128]{1,0:T(8,128)S(1)}, u32[]{:S(2)}, u32[]{:S(2)}) collective-permute-start(f32[136,128]{1,0:T(8,128)S(1)} %get-tuple-element.45), channel_id=1, source_target_pairs={{0,48},{4,52},{8,56},{12,60},{16,0},{20,4},{24,8},{28,12},{32,16},... | collective-permute-start | bytes 208904 | tf_op jit(solution)/shard_map/ppermute | solution.py:515
  85.7 1.9 %collective-permute-done.11.rest_5_ = f32[136,128]{1,0:T(8,128)S(1)} collective-permute-done((f32[136,128]{1,0:T(8,128)S(1)}, f32[136,128]{1,0:T(8,128)S(1)}, u32[]{:S(2)}, u32[]{:S(2)}) %collective-permute-start.11) | collective-permute-done | bytes 69664 | tf_op jit(solution)/shard_map/ppermute | solution.py:515
  87.6 2.0 %assemble.1 = f32[256,1024]{1,0:T(8,128)} custom-call(s32[2]{0:T(128)S(1)} %pad_add_fusion.where_ref, f32[2,128,128]{2,1,0:T(8,128)S(1)} %get-tuple-element.29.own_ref, f32[136,128]{1,0:T(8,128)S(1)} %get-tuple-element.38.rest_0_, f32[272,128]{1,0:T(8,128)S(1)} %collective-permute-done.7.up_ref.rest_1_, ...), custom_call_target="tpu_custom_call" | custom-call | tf_op jit(solution)/shard_map/assemble/pallas_call | solution.py:486
  (17 shorter events, 0.0 us)
Async XLA Ops:
  0.7 1.6 %copy-start.2 = (f32[1,2,512,512]{3,2,1,0:T(8,128)S(1)}, f32[1,2,512,512]{3,2,1,0:T(8,128)}, u32[]{:S(2)}) copy-start(f32[1,2,512,512]{3,2,1,0:T(8,128)} %param.6) | copy-start | bytes 6291460
  2.3 1.0 %copy-start.3 = (f32[1,2,128,384]{3,2,1,0:T(8,128)S(1)}, f32[1,2,128,384]{3,2,1,0:T(8,128)}, u32[]{:S(2)}) copy-start(f32[1,2,128,384]{3,2,1,0:T(8,128)} %param.8) | copy-start | bytes 1179652
  3.3 0.7 copy-start.4
  4.0 28.8 %copy-start = (s32[64,128]{1,0:T(8,128)S(1)}, s32[64,128]{1,0:T(8,128)}, u32[]{:S(2)}) copy-start(s32[64,128]{1,0:T(8,128)} %constant.11.clone.table_ref) | copy-start | bytes 98308
  4.0 28.8 %copy-start.1 = (bf16[1,2,512,16,128]{4,3,2,1,0:T(8,128)(2,1)S(1)}, bf16[1,2,512,16,128]{4,3,2,1,0:T(8,128)(2,1)}, u32[]{:S(2)}) copy-start(bf16[1,2,512,16,128]{4,3,2,1,0:T(8,128)(2,1)} %param.9) | copy-start | bytes 12582916
  4.0 28.8 %copy-start.5 = (s32[1,2,16]{2,1,0:T(2,128)S(1)}, s32[1,2,16]{2,1,0:T(2,128)}, u32[]{:S(2)}) copy-start(s32[1,2,16]{2,1,0:T(2,128)} %param.10) | copy-start | bytes 388
  40.9 7.6 %collective-permute-start = (f32[200,128]{1,0:T(8,128)S(1)}, f32[200,128]{1,0:T(8,128)S(1)}, u32[]{:S(2)}, u32[]{:S(2)}) collective-permute-start(f32[200,128]{1,0:T(8,128)S(1)} %get-tuple-element.31), channel_id=1, source_target_pairs={{0,4},{4,0},{8,12},{12,8},{16,20},{20,16},{24,28},{28,24},{32,36},... | collective-permute-start | bytes 307208 | tf_op jit(solution)/shard_map/ppermute | solution.py:515
  41.0 6.3 %collective-permute-start.2 = (f32[136,128]{1,0:T(8,128)S(1)}, f32[136,128]{1,0:T(8,128)S(1)}, u32[]{:S(2)}, u32[]{:S(2)}) collective-permute-start(f32[136,128]{1,0:T(8,128)S(1)} %get-tuple-element.33), channel_id=1, source_target_pairs={{0,68},{4,64},{8,76},{12,72},{16,84},{20,80},{24,92},{28,88},{32,1... | collective-permute-start | bytes 208904 | tf_op jit(solution)/shard_map/ppermute | solution.py:515
  42.6 13.9 %collective-permute-start.6 = (f32[200,128]{1,0:T(8,128)S(1)}, f32[200,128]{1,0:T(8,128)S(1)}, u32[]{:S(2)}, u32[]{:S(2)}) collective-permute-start(f32[200,128]{1,0:T(8,128)S(1)} %get-tuple-element.37), channel_id=1, source_target_pairs={{0,196},{4,192},{8,204},{12,200},{16,212},{20,208},{24,220},{28,21... | collective-permute-start | bytes 307208 | tf_op jit(solution)/shard_map/ppermute | solution.py:515
  44.1 13.9 %collective-permute-start.1 = (f32[264,128]{1,0:T(8,128)S(1)}, f32[264,128]{1,0:T(8,128)S(1)}, u32[]{:S(2)}, u32[]{:S(2)}) collective-permute-start(f32[264,128]{1,0:T(8,128)S(1)} %get-tuple-element.32), channel_id=1, source_target_pairs={{0,64},{4,68},{8,72},{12,76},{16,80},{20,84},{24,88},{28,92},{32,9... | collective-permute-start | bytes 405512 | tf_op jit(solution)/shard_map/ppermute | solution.py:515
  44.4 16.5 %collective-permute-start.3 = (f32[264,128]{1,0:T(8,128)S(1)}, f32[264,128]{1,0:T(8,128)S(1)}, u32[]{:S(2)}, u32[]{:S(2)}) collective-permute-start(f32[264,128]{1,0:T(8,128)S(1)} %get-tuple-element.34), channel_id=1, source_target_pairs={{0,128},{4,132},{8,136},{12,140},{16,144},{20,148},{24,152},{28,15... | collective-permute-start | bytes 405512 | tf_op jit(solution)/shard_map/ppermute | solution.py:515
  47.3 14.0 %collective-permute-start.4 = (f32[264,128]{1,0:T(8,128)S(1)}, f32[264,128]{1,0:T(8,128)S(1)}, u32[]{:S(2)}, u32[]{:S(2)}) collective-permute-start(f32[264,128]{1,0:T(8,128)S(1)} %get-tuple-element.35), channel_id=1, source_target_pairs={{0,132},{4,128},{8,140},{12,136},{16,148},{20,144},{24,156},{28,15... | collective-permute-start | bytes 405512 | tf_op jit(solution)/shard_map/ppermute | solution.py:515
  48.4 12.9 %collective-permute-start.5 = (f32[264,128]{1,0:T(8,128)S(1)}, f32[264,128]{1,0:T(8,128)S(1)}, u32[]{:S(2)}, u32[]{:S(2)}) collective-permute-start(f32[264,128]{1,0:T(8,128)S(1)} %get-tuple-element.36), channel_id=1, source_target_pairs={{0,192},{4,196},{8,200},{12,204},{16,208},{20,212},{24,216},{28,22... | collective-permute-start | bytes 405512 | tf_op jit(solution)/shard_map/ppermute | solution.py:515
  56.5 29.2 %collective-permute-start.12 = (f32[2,328,128]{2,1,0:T(8,128)S(1)}, f32[2,328,128]{2,1,0:T(8,128)S(1)}, u32[]{:S(2)}, u32[]{:S(2)}) collective-permute-start(f32[2,328,128]{2,1,0:T(8,128)S(1)} %get-tuple-element.47.rest_7_), channel_id=1, source_target_pairs={{0,1},{1,2},{2,3},{3,0},{4,5},{5,6},{6,7},{7,4},{8,9},{9,10},{10,1... | collective-permute-start | bytes 1007624 | tf_op jit(solution)/shard_map/ppermute | solution.py:522
  58.0 27.7 %collective-permute-start.13 = (f32[2,328,128]{2,1,0:T(8,128)S(1)}, f32[2,328,128]{2,1,0:T(8,128)S(1)}, u32[]{:S(2)}, u32[]{:S(2)}) collective-permute-start(f32[2,328,128]{2,1,0:T(8,128)S(1)} %get-tuple-element.48.rest_8_), channel_id=1, source_target_pairs={{0,2},{1,3},{2,0},{3,1},{4,6},{5,7},{6,4},{7,5},{8,10},{9,11},{10,... | collective-permute-start | bytes 1007624 | tf_op jit(solution)/shard_map/ppermute | solution.py:522
  60.9 24.9 %collective-permute-start.14 = (f32[2,328,128]{2,1,0:T(8,128)S(1)}, f32[2,328,128]{2,1,0:T(8,128)S(1)}, u32[]{:S(2)}, u32[]{:S(2)}) collective-permute-start(f32[2,328,128]{2,1,0:T(8,128)S(1)} %get-tuple-element.49.rest_9_), channel_id=1, source_target_pairs={{0,3},{1,0},{2,1},{3,2},{4,7},{5,4},{6,5},{7,6},{8,11},{9,8},{10,9... | collective-permute-start | bytes 1007624 | tf_op jit(solution)/shard_map/ppermute | solution.py:522
  62.8 9.4 %collective-permute-start.7 = (f32[272,128]{1,0:T(8,128)S(1)}, f32[272,128]{1,0:T(8,128)S(1)}, u32[]{:S(2)}, u32[]{:S(2)}) collective-permute-start(f32[272,128]{1,0:T(8,128)S(1)} %get-tuple-element.39), channel_id=1, source_target_pairs={{0,8},{4,12},{8,16},{12,20},{16,24},{20,28},{24,32},{28,36},{32,40... | collective-permute-start | bytes 417800 | tf_op jit(solution)/shard_map/ppermute | solution.py:515
  64.8 11.7 %collective-permute-start.8 = (f32[272,128]{1,0:T(8,128)S(1)}, f32[272,128]{1,0:T(8,128)S(1)}, u32[]{:S(2)}, u32[]{:S(2)}) collective-permute-start(f32[272,128]{1,0:T(8,128)S(1)} %get-tuple-element.40), channel_id=1, source_target_pairs={{0,56},{4,60},{8,0},{12,4},{16,8},{20,12},{24,16},{28,20},{32,24},... | collective-permute-start | bytes 417800 | tf_op jit(solution)/shard_map/ppermute | solution.py:515
  72.2 9.4 %collective-permute-start.9 = (f32[136,128]{1,0:T(8,128)S(1)}, f32[136,128]{1,0:T(8,128)S(1)}, u32[]{:S(2)}, u32[]{:S(2)}) collective-permute-start(f32[136,128]{1,0:T(8,128)S(1)} %get-tuple-element.41), channel_id=1, source_target_pairs={{0,32},{4,36},{8,40},{12,44},{16,48},{20,52},{24,56},{28,60},{32,0... | collective-permute-start | bytes 208904 | tf_op jit(solution)/shard_map/ppermute | solution.py:515
  76.5 9.2 %collective-permute-start.10 = (f32[136,128]{1,0:T(8,128)S(1)}, f32[136,128]{1,0:T(8,128)S(1)}, u32[]{:S(2)}, u32[]{:S(2)}) collective-permute-start(f32[136,128]{1,0:T(8,128)S(1)} %get-tuple-element.44), channel_id=1, source_target_pairs={{0,16},{4,20},{8,24},{12,28},{16,32},{20,36},{24,40},{28,44},{32,4... | collective-permute-start | bytes 208904 | tf_op jit(solution)/shard_map/ppermute | solution.py:515
  81.7 6.0 %collective-permute-start.11 = (f32[136,128]{1,0:T(8,128)S(1)}, f32[136,128]{1,0:T(8,128)S(1)}, u32[]{:S(2)}, u32[]{:S(2)}) collective-permute-start(f32[136,128]{1,0:T(8,128)S(1)} %get-tuple-element.45), channel_id=1, source_target_pairs={{0,48},{4,52},{8,56},{12,60},{16,0},{20,4},{24,8},{28,12},{32,16},... | collective-permute-start | bytes 208904 | tf_op jit(solution)/shard_map/ppermute | solution.py:515
where the time goes:
time: 89.8 us; the launch traced here: 89.7 us
  Pallas kernels  46.7 us (52%)
  starting transfers between devices  28.8 us (32%)
  waiting for transfers between devices  10.1 us (11%)
  local copies, waits for them, and re-layouts  3.28 us (4%)
    pallas_call x1, Pallas kernels, factor(): pl.pallas_call(factor_kernel, out_shape=(jax.ShapeDtypeStruct((count, dof...  28.8 us
    ppermute x12, starting transfers between devices, shifted(): return lax.ppermute(block, 'box', moves)  24 us
    ppermute x12, waiting for transfers between devices, shifted(): return lax.ppermute(block, 'box', moves)  10.1 us
    pallas_call x1, Pallas kernels, far_updates(): pl.pallas_call(functools.partial(far_kernel, caps=caps, starts=starts, bo...  8.05 us
    pallas_call x1, Pallas kernels, near_updates(): pl.pallas_call(near_kernel, out_shape=[jax.ShapeDtypeStruct((count, skel,...  6.28 us
    ppermute x3, starting transfers between devices, on_device(): lax.ppermute(kept[s], 'sib', [(i, (i + s) % sibs) for i in range(sibs)])  4.76 us
    unnamed x12, local copies, waits for them, and re-layouts  3.28 us
    pallas_call x1, Pallas kernels, assemble(): pl.pallas_call(assemble_kernel, out_shape=jax.ShapeDtypeStruct((256, 1024...  2.01 us
  transfers between devices with their start and end apart: 15, of which 3 were waited for; matrix products, arithmetic and copies ran while one was open for 0% of the time, Pallas kernels for 9%

commit v1 on v0

--- a/solution.py
+++ b/solution.py
@@ -44,11 +44,12 @@
     return jnp.take_along_axis(x, jnp.full(x.shape, lane, jnp.int32), axis=1)
 
 
-def eliminate_rows(panels, base):
+def eliminate_rows(panels, nexts, base):
     shape = panels[0].shape
     lane, sub = iota(shape, 1), iota(shape, 0)
-    panels = list(panels)
+    panels, nexts = list(panels), list(nexts)
     columns = [[spread(panel, base + t) for t in range(8)] for panel in panels]
+    next_columns = [[spread(rows, base + t) for t in range(8)] for rows in nexts]
     inverses = [jnp.ones(shape, F32) for _ in panels]
     for t in range(8):
         here = lane == base + t
@@ -58,17 +59,25 @@
             inverse = 1.0 / jnp.broadcast_to(column[t : t + 1, :], shape)
             inverses[b] = jnp.where(sub == t, inverse, inverses[b])
             ratio = jnp.where(sub > t, column, 0.0) * inverse
+            row = jnp.where(here, 1.0, jnp.broadcast_to(panel[t : t + 1, :], shape))
+            if nexts:
+                next_ratio = next_columns[b][t] * inverse
             for u in range(t + 1, 8):
                 later = columns[b][u]
-                columns[b][u] = later - ratio * jnp.broadcast_to(later[t : t + 1, :], shape)
-            row = jnp.where(here, 1.0, jnp.broadcast_to(panel[t : t + 1, :], shape))
+                pivot_row = jnp.broadcast_to(later[t : t + 1, :], shape)
+                columns[b][u] = later - ratio * pivot_row
+                if nexts:
+                    next_columns[b][u] = next_columns[b][u] - next_ratio * pivot_row
             panels[b] = jnp.where(here, one, panel) - ratio * row
-    return panels, inverses
+            if nexts:
+                nexts[b] = jnp.where(here, 0.0, nexts[b]) - next_ratio * row
+    return panels, nexts, inverses
 
 
 def invert_cholesky(blocks):
     count, size, span = len(blocks), blocks[0].shape[0], 32
-    lane, sub = iota((8, size), 1), iota((8, size), 0)
+    shape = (8, size)
+    lane, sub = iota(shape, 1), iota(shape, 0)
     rows = [[block[8 * g : 8 * g + 8, :] for g in range(size // 8)] for block in blocks]
     out = [[] for _ in blocks]
     for start in range(0, size, span):
@@ -76,7 +85,8 @@
         finals, scaled_rows = [[] for _ in blocks], [[] for _ in blocks]
         for g in range(start // 8, end // 8):
             base = 8 * g
-            panels, inverses = eliminate_rows([rows[b][g] for b in range(count)], base)
+            nexts = [rows[b][g + 1] for b in range(count)] if base + 8 < end else []
+            panels, nexts, inverses = eliminate_rows([r[g] for r in rows], nexts, base)
             for b in range(count):
                 panel = panels[b]
                 scaled = panel * inverses[b]
@@ -84,16 +94,17 @@
                 out[b].append(jnp.where(beyond, 0.0, panel * jnp.sqrt(inverses[b])))
                 finals[b].append(panel)
                 scaled_rows[b].append(jnp.where(beyond & (lane < end), 0.0, scaled))
-                if base + 8 == end:
+                if not nexts:
                     continue
+                rows[b][g + 1] = nexts[b]
                 scaled = jnp.where(beyond & (lane < base + 8), 0.0, scaled)
-                flipped = panel.T
                 clear = (lane >= base) & (lane < base + 8)
-                for i in range(g + 1, end // 8):
-                    factors = flipped[8 * i : 8 * i + 8, :]
+                for i in range(g + 2, end // 8):
                     terms = [
-                        jnp.broadcast_to(factors[:, t : t + 1], (8, size))
-                        * jnp.broadcast_to(scaled[t : t + 1, :], (8, size))
+                        jnp.take_along_axis(
+                            jnp.broadcast_to(panel[t : t + 1, :], shape), 8 * i + sub, axis=1
+                        )
+                        * jnp.broadcast_to(scaled[t : t + 1, :], shape)
                         for t in range(8)
                     ]
                     while len(terms) > 1:
@@ -110,22 +121,63 @@
     return [jnp.concatenate(parts, axis=0) for parts in out]
 
 
-def factor_kernel(blocks_ref, orders_ref, interp_ref, high_ref, low_ref, own_ref, work, aug):
+def pick_lanes(x, order):
+    rows, width = x.shape
+    chunks = [x[:, 128 * q : 128 * (q + 1)] for q in range(width // 128)]
+    parts = []
+    for q in range(width // 128):
+        wanted = jnp.broadcast_to(order[:, 128 * q : 128 * (q + 1)], (rows, 128))
+        lane, chunk = wanted & 127, wanted >> 7
+        picked = jnp.take_along_axis(chunks[0], lane, axis=1)
+        for c in range(1, len(chunks)):
+            picked = jnp.where(chunk == c, jnp.take_along_axis(chunks[c], lane, axis=1), picked)
+        parts.append(picked)
+    return jnp.concatenate(parts, axis=1)
+
+
+def one_hot_rows(order, rows, width):
+    column = jnp.broadcast_to(order.astype(F32), (128, order.shape[1])).T
+    lanes = iota((rows, 128), 1).astype(F32)
+    return jnp.concatenate(
+        [(column[:rows] == lanes + 128.0 * q).astype(F32) for q in range(width // 128)], axis=1
+    )
+
+
+def factor_kernel(
+    blocks_hbm,
+    orders_hbm,
+    interp_hbm,
+    high_ref,
+    low_ref,
+    own_ref,
+    blocks_ref,
+    orders_ref,
+    interp_ref,
+    work,
+    aug,
+    sems,
+):
     count, dof, _ = blocks_ref.shape
     skel, red = interp_ref.shape[1:]
+    order_copy = pltpu.make_async_copy(orders_hbm, orders_ref, sems.at[0])
+    block_copy = lambda b: pltpu.make_async_copy(
+        blocks_hbm.at[b], blocks_ref.at[b], sems.at[1 + b]
+    )
+    interp_copy = lambda b: pltpu.make_async_copy(
+        interp_hbm.at[b], interp_ref.at[b], sems.at[1 + count + b]
+    )
+    order_copy.start()
     for b in range(count):
-        order = orders_ref[b : b + 1, :]
-        place_t = (iota((dof, dof), 0) == order).astype(F32).astype(BF16)
-        column = jnp.broadcast_to(order.astype(F32), (128, dof)).T
-        lanes = iota((dof, 128), 1).astype(F32)
-        place = jnp.concatenate(
-            [(column == lanes + 128.0 * q).astype(F32) for q in range(dof // 128)], axis=1
-        )
-        place_b = place.astype(BF16)
-        parts = [dot_bf16(place_b, part).astype(BF16) for part in split3(blocks_ref[b])]
-        ordered = dot_bf16(parts[0], place_t) + (
-            dot_bf16(parts[1], place_t) + dot_bf16(parts[2], place_t)
-        )
+        block_copy(b).start()
+        interp_copy(b).start()
+    order_copy.wait()
+
+    @pl.loop(0, count)
+    def _(b):
+        order = orders_ref[pl.ds(b, 1), :]
+        block_copy(b).wait()
+        ordered = pick_lanes(pick_lanes(blocks_ref[b], order).T, order)
+        interp_copy(b).wait()
         a_ss = ordered[:skel, :skel]
         a_sr = ordered[:skel, skel:]
         interp = interp_ref[b]
@@ -134,10 +186,13 @@
         left = jnp.concatenate([a_sr.T, interp_t], axis=1)
         right = jnp.concatenate([interp, bar_sr], axis=0)
         work[b] = ordered[skel:, skel:] - dot_high(left, right)
-        pieces = [dot_bf16(part, place_b[:skel]) for part in split3(interp_t)]
+        place = one_hot_rows(order, dof, dof)
+        place_s = place[:skel].astype(BF16)
+        pieces = [dot_bf16(part, place_s) for part in split3(interp_t)]
         aug[b, :, :dof] = place[skel:] - (pieces[0] + (pieces[1] + pieces[2]))
         aug[b, :, dof:] = bar_sr.T
         own_ref[b] = a_ss
+
     panels = red // 128
     for k in range(panels):
         lo, hi = 128 * k, 128 * (k + 1)
@@ -155,11 +210,7 @@
         grid_high, grid_low = split2(aug[b, :, :dof])
         high_ref[b, :red] = grid_high
         low_ref[b, :red] = grid_low
-        column = jnp.broadcast_to(orders_ref[b : b + 1, :].astype(F32), (128, dof)).T
-        lanes = iota((skel, 128), 1).astype(F32)
-        place_s = jnp.concatenate(
-            [(column[:skel] == lanes + 128.0 * q).astype(F32) for q in range(dof // 128)], axis=1
-        )
+        place_s = one_hot_rows(orders_ref[b : b + 1, :], skel, dof)
         last_high, last_low = split2(place_s - dot_high(solved_t, aug[b, :, :dof]))
         high_ref[b, red:] = last_high
         low_ref[b, red:] = last_low
@@ -175,8 +226,16 @@
             jax.ShapeDtypeStruct((count, dof, dof), BF16),
             jax.ShapeDtypeStruct((count, skel, skel), F32),
         ),
-        scratch_shapes=[pltpu.VMEM((count, red, red), F32), pltpu.VMEM((count, red, dof + skel), F32)],
-        compiler_params=pltpu.CompilerParams(vmem_limit_bytes=24 << 20),
+        in_specs=[pl.BlockSpec(memory_space=pltpu.HBM)] * 3,
+        scratch_shapes=[
+            pltpu.VMEM((count, dof, dof), F32),
+            pltpu.VMEM((count, dof), jnp.int32),
+            pltpu.VMEM((count, skel, red), F32),
+            pltpu.VMEM((count, red, red), F32),
+            pltpu.VMEM((count, red, dof + skel), F32),
+            pltpu.SemaphoreType.DMA((2 * count + 1,)),
+        ],
+        compiler_params=pltpu.CompilerParams(vmem_limit_bytes=51 << 20),
         cost_estimate=pl.CostEstimate(flops=8 << 30, bytes_accessed=6 << 20, transcendentals=0),
         interpret=interpret,
         name="factor",
@@ -318,34 +377,33 @@
     )(ids, where, table, high, low, w)
 
 
-def near_kernel(ids_ref, where_ref, high_ref, low_ref, last_high_ref, last_low_ref, w_ref, *rest):
-    updated_ref, sib_outs, sib = rest[0], rest[1:-1], rest[-1]
+def near_kernel(ids_ref, where_ref, high_ref, low_ref, w_ref, *rest):
+    near_ref, sib_outs, sib = rest[0], rest[1:-1], rest[-1]
     box = pl.program_id(0)
     this_sib = where_ref[1]
+    red = high_ref.shape[1] - w_ref.shape[3]
 
     @pl.when(box == 0)
     def _():
         sib[...] = jnp.zeros_like(sib)
 
-    slots = w_ref.shape[2]
-    by_slot = jnp.swapaxes(w_ref[0], 0, 1)
-    coupled_slots = []
-    for first in range(0, slots, 2):
+    by_slot = jnp.swapaxes(w_ref[0, :, :8], 0, 1)
+    for first in range(0, NSIB, 2):
         pair = jnp.concatenate([by_slot[first], by_slot[first + 1]], axis=1)
-        coupled = dot_bf16(last_high_ref[0], pair) + dot_bf16(last_low_ref[0], pair)
-        coupled_slots += [coupled[:, :128].astype(BF16), coupled[:, 128:].astype(BF16)]
-        if first >= NSIB:
-            continue
-        for s, update in enumerate(slot_updates(high_ref, low_ref, pair)):
+        product = dot_bf16(high_ref[0], pair) + dot_bf16(low_ref[0], pair)
+        both = gram(product[:red].T)
+        for s in range(2):
+            part = slice(128 * s, 128 * (s + 1))
+            coupled = product[red:, part]
+            near_ref[0, first + s] = coupled
             other = ids_ref[box, first + s]
             child = other & 1
-            body, tail = pack_symmetric(update, child.astype(F32))
+            body, tail = pack_symmetric(both[part, part], child.astype(F32))
             place = ((((other >> 1) & 3) - this_sib) & 3) * 2 + child
             rows = pl.ds(pl.multiple_of(box * 128, 128), 128)
-            sib[place, rows, :] = coupled[:, 128 * s : 128 * s + 128]
+            sib[place, rows, :] = coupled
             sib[place, 256:320, :] = sib[place, 256:320, :] + body
             sib[place, 320:321, :] = sib[place, 320:321, :] + tail
-    updated_ref[0] = jnp.swapaxes(jnp.stack(coupled_slots), 0, 1)
 
     @pl.when(box == pl.num_programs(0) - 1)
     def _():
@@ -355,26 +413,18 @@
 
 def near_updates(ids, where, high, low, w, interpret=False):
     count, dof, slots, skel = w.shape
-    red = dof - skel
     by_box = lambda shape: pl.BlockSpec((1,) + shape, lambda b, *_: (b,) + (0,) * len(shape))
-    last = pl.BlockSpec((1, skel, dof), lambda b, *_: (b, red // skel, 0))
     return pl.pallas_call(
         near_kernel,
         out_shape=(
-            [jax.ShapeDtypeStruct((count, skel, slots, skel), BF16)]
+            [jax.ShapeDtypeStruct((count, NSIB, skel, skel), F32)]
             + [jax.ShapeDtypeStruct((2, 328, 128), F32)] * 4
         ),
         grid_spec=pltpu.PrefetchScalarGridSpec(
             num_scalar_prefetch=2,
             grid=(count,),
-            in_specs=[
-                by_box((red, dof)),
-                by_box((red, dof)),
-                last,
-                last,
-                by_box((dof, slots, skel)),
-            ],
-            out_specs=[by_box((skel, slots, skel))]
+            in_specs=[by_box((dof, dof)), by_box((dof, dof)), by_box((dof, slots, skel))],
+            out_specs=[by_box((NSIB, skel, skel))]
             + [pl.BlockSpec((2, 328, 128), lambda b, *_: (0, 0, 0))] * 4,
             scratch_shapes=[pltpu.VMEM((8, 328, 128), F32)],
         ),
@@ -382,7 +432,35 @@
         cost_estimate=pl.CostEstimate(flops=3 << 30, bytes_accessed=8 << 20, transcendentals=0),
         interpret=interpret,
         name="near_updates",
-    )(ids, where, high, low, high, low, w)
+    )(ids, where, high, low, w)
+
+
+def couple_kernel(high_ref, low_ref, near_ref, w_ref, updated_ref):
+    slots = w_ref.shape[2]
+    by_slot = jnp.swapaxes(w_ref[0], 0, 1)
+    parts = [near_ref[0, k].astype(BF16) for k in range(NSIB)]
+    for first in range(NSIB, slots, 2):
+        pair = jnp.concatenate([by_slot[first], by_slot[first + 1]], axis=1)
+        coupled = dot_bf16(high_ref[0], pair) + dot_bf16(low_ref[0], pair)
+        parts += [coupled[:, :128].astype(BF16), coupled[:, 128:].astype(BF16)]
+    updated_ref[0] = jnp.swapaxes(jnp.stack(parts), 0, 1)
+
+
+def couple(high, low, near, w, interpret=False):
+    count, dof, slots, skel = w.shape
+    by_box = lambda shape: pl.BlockSpec((1,) + shape, lambda b: (b,) + (0,) * len(shape))
+    last = pl.BlockSpec((1, skel, dof), lambda b: (b, dof // skel - 1, 0))
+    return pl.pallas_call(
+        couple_kernel,
+        out_shape=jax.ShapeDtypeStruct((count, skel, slots, skel), BF16),
+        grid=(count,),
+        in_specs=[last, last, by_box((NSIB, skel, skel)), by_box((dof, slots, skel))],
+        out_specs=by_box((skel, slots, skel)),
+        compiler_params=pltpu.CompilerParams(vmem_limit_bytes=28 << 20),
+        cost_estimate=pl.CostEstimate(flops=2 << 30, bytes_accessed=6 << 20, transcendentals=0),
+        interpret=interpret,
+        name="couple",
+    )(high, low, near, w)
 
 
 def route_kernel(where_ref, table_ref, *rest, caps, starts, boxes):
@@ -517,17 +595,20 @@
     got = [sent[0]]
     for (dy, dc), block in zip(STAGES[1:], sent[1:]):
         got.append(shifted(block, dy, 0, dc))
-    updated, *kept = near_updates(ids, where, high, low, couplings[0])
-    sib_got = [
-        lax.ppermute(kept[s], "sib", [(i, (i + s) % sibs) for i in range(sibs)])
-        for s in range(1, sibs)
-    ]
+    near, *kept = near_updates(ids, where, high, low, couplings[0])
+    sib_got = []
+    for s in range(1, sibs):
+        moves = [(i, (i + s) % sibs) for i in range(sibs)]
+        sib_got.append(lax.ppermute(kept[s], "sib", moves))
     here, up, down, four, two, six = route(where, table, got, caps, starts, boxes)
     up = shifted(up, 0, 1, 0)
     down = shifted(down, 0, -1, 0)
     four = shifted(four, 0, 4, 0)
     two, six = fold(up, down, two, six)
-    far = [here, up, down, four, shifted(two, 0, 2, 0), shifted(six, 0, -2, 0)]
+    two = shifted(two, 0, 2, 0)
+    six = shifted(six, 0, -2, 0)
+    far = [here, up, down, four, two, six]
+    updated = couple(high, low, near, couplings[0])
     rows = assemble(where, own, far, kept, sib_got)
     return updated[None], rows[None]
 

time: 89.8 us -> 92 us (1.024)
  the two profiles are of different devices: /device:TPU:2 before, /device:TPU:8 now
where the time goes in v1:
time: 92 us; the launch traced here: 91.9 us
  Pallas kernels  46.4 us (50%)
  starting transfers between devices  29 us (32%)
  waiting for transfers between devices  13.9 us (15%)
  local copies, waits for them, and re-layouts  1.69 us (2%)
    pallas_call x1, Pallas kernels, factor(): pl.pallas_call(factor_kernel, out_shape=(jax.ShapeDtypeStruct((count, dof...  26.1 us
    ppermute x12, starting transfers between devices, shifted(): return lax.ppermute(block, 'box', moves)  23 us
    ppermute x12, waiting for transfers between devices, shifted(): return lax.ppermute(block, 'box', moves)  13.9 us
    pallas_call x1, Pallas kernels, far_updates(): pl.pallas_call(functools.partial(far_kernel, caps=caps, starts=starts, bo...  8.08 us
    ppermute x3, starting transfers between devices, on_device(): sib_got.append(lax.ppermute(kept[s], 'sib', moves))  6 us
    pallas_call x1, Pallas kernels, near_updates(): pl.pallas_call(near_kernel, out_shape=[jax.ShapeDtypeStruct((count, NSIB,...  5.7 us
    pallas_call x1, Pallas kernels, couple(): pl.pallas_call(couple_kernel, out_shape=jax.ShapeDtypeStruct((count, skel...  2.95 us
    pallas_call x1, Pallas kernels, assemble(): pl.pallas_call(assemble_kernel, out_shape=jax.ShapeDtypeStruct((256, 1024...  2.01 us
  transfers between devices with their start and end apart: 15, of which 2 were waited for; matrix products, arithmetic and copies ran while one was open for 0% of the time, Pallas kernels for 9%

profile of v1, /device:TPU:8, one launch (start us, length us, event | category | flops | bytes accessed | tf_op | source)
XLA Modules:
  0.0 91.9 jit_solution(4785535575010733861)
XLA Ops:
  0.6 0.1 pad_add_fusion.where_ref
  0.7 1.0 %copy-done.2 = f32[1,2,128,384]{3,2,1,0:T(8,128)S(1)} copy-done((f32[1,2,128,384]{3,2,1,0:T(8,128)S(1)}, f32[1,2,128,384]{3,2,1,0:T(8,128)}, u32[]{:S(2)}) %copy-start.2) | copy-done | bytes 393240
  1.7 0.7 copy-done.3
  2.4 26.1 %factor.1 = (bf16[2,512,512]{2,1,0:T(8,128)(2,1)S(1)}, bf16[2,512,512]{2,1,0:T(8,128)(2,1)S(1)}, f32[2,128,128]{2,1,0:T(8,128)S(1)}) custom-call(f32[2,512,512]{2,1,0:T(8,128)} %bitcast.17, s32[2,512]{1,0:T(2,128)S(1)} %bitcast.13, f32[2,128,384]{2,1,0:T(8,128)S(1)} %bitcast.12), custom_call_target="tpu_custom_call" | custom-call | flops 8589934592 | bytes 6291456 | tf_op jit(solution)/shard_map/factor/pallas_call | solution.py:222
  28.6 8.1 %far_updates.1 = (f32[264,128]{1,0:T(8,128)S(1)}, f32[200,128]{1,0:T(8,128)S(1)}, f32[264,128]{1,0:T(8,128)S(1)}, f32[136,128]{1,0:T(8,128)S(1)}, f32[264,128]{1...) custom-call(s32[2,16]{1,0:T(2,128)S(1)} %bitcast.14, ...), custom_call_target="tpu_custom_call" | custom-call | flops 6442450944 | bytes 8388608 | tf_op jit(solution)/shard_map/far_updates/pallas_call | solution.py:359
  36.6 0.1 collective-permute-start
  36.7 1.7 %collective-permute-start.2 = (f32[136,128]{1,0:T(8,128)S(1)}, f32[136,128]{1,0:T(8,128)S(1)}, u32[]{:S(2)}, u32[]{:S(2)}) collective-permute-start(f32[136,128]{1,0:T(8,128)S(1)} %get-tuple-element.33), channel_id=1, source_target_pairs={{0,68},{4,64},{8,76},{12,72},{16,84},{20,80},{24,92},{28,88},{32,1... | collective-permute-start | bytes 208904 | tf_op jit(solution)/shard_map/ppermute | solution.py:593
  38.4 1.3 %collective-permute-start.1 = (f32[264,128]{1,0:T(8,128)S(1)}, f32[264,128]{1,0:T(8,128)S(1)}, u32[]{:S(2)}, u32[]{:S(2)}) collective-permute-start(f32[264,128]{1,0:T(8,128)S(1)} %get-tuple-element.32), channel_id=1, source_target_pairs={{0,64},{4,68},{8,72},{12,76},{16,80},{20,84},{24,88},{28,92},{32,9... | collective-permute-start | bytes 405512 | tf_op jit(solution)/shard_map/ppermute | solution.py:593
  39.7 1.4 %collective-permute-start.3 = (f32[264,128]{1,0:T(8,128)S(1)}, f32[264,128]{1,0:T(8,128)S(1)}, u32[]{:S(2)}, u32[]{:S(2)}) collective-permute-start(f32[264,128]{1,0:T(8,128)S(1)} %get-tuple-element.34), channel_id=1, source_target_pairs={{0,128},{4,132},{8,136},{12,140},{16,144},{20,148},{24,152},{28,15... | collective-permute-start | bytes 405512 | tf_op jit(solution)/shard_map/ppermute | solution.py:593
  41.1 1.2 %collective-permute-start.4 = (f32[264,128]{1,0:T(8,128)S(1)}, f32[264,128]{1,0:T(8,128)S(1)}, u32[]{:S(2)}, u32[]{:S(2)}) collective-permute-start(f32[264,128]{1,0:T(8,128)S(1)} %get-tuple-element.35), channel_id=1, source_target_pairs={{0,132},{4,128},{8,140},{12,136},{16,148},{20,144},{24,156},{28,15... | collective-permute-start | bytes 405512 | tf_op jit(solution)/shard_map/ppermute | solution.py:593
  42.4 0.0 collective-permute-done.2.rest_3_
  42.4 1.7 %collective-permute-start.5 = (f32[264,128]{1,0:T(8,128)S(1)}, f32[264,128]{1,0:T(8,128)S(1)}, u32[]{:S(2)}, u32[]{:S(2)}) collective-permute-start(f32[264,128]{1,0:T(8,128)S(1)} %get-tuple-element.36), channel_id=1, source_target_pairs={{0,192},{4,196},{8,200},{12,204},{16,208},{20,212},{24,216},{28,22... | collective-permute-start | bytes 405512 | tf_op jit(solution)/shard_map/ppermute | solution.py:593
  44.1 0.0 collective-permute-done.rest_1_
  44.1 1.2 %collective-permute-start.6 = (f32[200,128]{1,0:T(8,128)S(1)}, f32[200,128]{1,0:T(8,128)S(1)}, u32[]{:S(2)}, u32[]{:S(2)}) collective-permute-start(f32[200,128]{1,0:T(8,128)S(1)} %get-tuple-element.37), channel_id=1, source_target_pairs={{0,196},{4,192},{8,204},{12,200},{16,212},{20,208},{24,220},{28,21... | collective-permute-start | bytes 307208 | tf_op jit(solution)/shard_map/ppermute | solution.py:593
  45.3 9.2 %collective-permute-done.6.rest_7_ = f32[200,128]{1,0:T(8,128)S(1)} collective-permute-done((f32[200,128]{1,0:T(8,128)S(1)}, f32[200,128]{1,0:T(8,128)S(1)}, u32[]{:S(2)}, u32[]{:S(2)}) %collective-permute-start.6) | collective-permute-done | bytes 102432 | tf_op jit(solution)/shard_map/ppermute | solution.py:593
  54.5 0.0 collective-permute-done.1.rest_2_
  54.5 0.0 collective-permute-done.3.rest_4_
  54.5 0.0 collective-permute-done.4.rest_5_
  54.5 0.0 collective-permute-done.5.rest_6_
  54.5 1.5 %route.1 = (f32[136,128]{1,0:T(8,128)S(1)}, f32[272,128]{1,0:T(8,128)S(1)}, f32[272,128]{1,0:T(8,128)S(1)}, f32[136,128]{1,0:T(8,128)S(1)}, f32[136,128]{1,0:T(8,128)S(1)}, /*index=5*/f32[136,128]{1,0:T(8,128)S(1)}) custom-call(s32[2]{0:T(128)S(1)} %pad_add_fusion.where_ref, s32[64,128]{1,0:T(8,128)S(1)} %copy-done, ...), custom_call_target="tpu_custom_call" | custom-call | flops 4194304 | bytes 2097152 | tf_op jit(solution)/shard_map/route/pallas_call | solution.py:494
  56.1 2.0 %collective-permute-start.7 = (f32[272,128]{1,0:T(8,128)S(1)}, f32[272,128]{1,0:T(8,128)S(1)}, u32[]{:S(2)}, u32[]{:S(2)}) collective-permute-start(f32[272,128]{1,0:T(8,128)S(1)} %get-tuple-element.39), channel_id=1, source_target_pairs={{0,8},{4,12},{8,16},{12,20},{16,24},{20,28},{24,32},{28,36},{32,40... | collective-permute-start | bytes 417800 | tf_op jit(solution)/shard_map/ppermute | solution.py:593
  58.1 4.0 %collective-permute-start.8 = (f32[272,128]{1,0:T(8,128)S(1)}, f32[272,128]{1,0:T(8,128)S(1)}, u32[]{:S(2)}, u32[]{:S(2)}) collective-permute-start(f32[272,128]{1,0:T(8,128)S(1)} %get-tuple-element.40), channel_id=1, source_target_pairs={{0,56},{4,60},{8,0},{12,4},{16,8},{20,12},{24,16},{28,20},{32,24},... | collective-permute-start | bytes 417800 | tf_op jit(solution)/shard_map/ppermute | solution.py:593
  62.1 5.7 %near_updates.1 = (f32[2,4,128,128]{3,2,1,0:T(8,128)S(1)}, f32[2,328,128]{2,1,0:T(8,128)S(1)}, f32[2,328,128]{2,1,0:T(8,128)S(1)}, f32[2,328,128]{2,1,0:T(8,128)S(1)}, f32[2,328,128]{2,1,0:T(8,128)S(1)}) custom-call(s32[2,16]{1,0:T(2,128)S(1)} %bitcast.15, s32[2]{0:T(128)S(1)} %pad_add_fusion.where_ref, bf16[2,512,512]{2,1,0:T(8,128)(2,1)S(1)} %get-tuple-element.26.high_ref, ...), custom_call_target="tpu_custom_call" | custom-call | flops 3221225472 | bytes 8388608 | tf_op jit(solution)/shard_map/near_updates/pallas_call | solution.py:417
  67.8 1.8 %collective-permute-start.12 = (f32[2,328,128]{2,1,0:T(8,128)S(1)}, f32[2,328,128]{2,1,0:T(8,128)S(1)}, u32[]{:S(2)}, u32[]{:S(2)}) collective-permute-start(f32[2,328,128]{2,1,0:T(8,128)S(1)} %get-tuple-element.47.rest_7_), channel_id=1, source_target_pairs={{0,1},{1,2},{2,3},{3,0},{4,5},{5,6},{6,7},{7,4},{8,9},{9,10},{10,1... | collective-permute-start | bytes 1007624 | tf_op jit(solution)/shard_map/ppermute | solution.py:602
  69.6 2.7 %collective-permute-start.13 = (f32[2,328,128]{2,1,0:T(8,128)S(1)}, f32[2,328,128]{2,1,0:T(8,128)S(1)}, u32[]{:S(2)}, u32[]{:S(2)}) collective-permute-start(f32[2,328,128]{2,1,0:T(8,128)S(1)} %get-tuple-element.48.rest_8_), channel_id=1, source_target_pairs={{0,2},{1,3},{2,0},{3,1},{4,6},{5,7},{6,4},{7,5},{8,10},{9,11},{10,... | collective-permute-start | bytes 1007624 | tf_op jit(solution)/shard_map/ppermute | solution.py:602
  72.4 1.4 %collective-permute-start.14 = (f32[2,328,128]{2,1,0:T(8,128)S(1)}, f32[2,328,128]{2,1,0:T(8,128)S(1)}, u32[]{:S(2)}, u32[]{:S(2)}) collective-permute-start(f32[2,328,128]{2,1,0:T(8,128)S(1)} %get-tuple-element.49.rest_9_), channel_id=1, source_target_pairs={{0,3},{1,0},{2,1},{3,2},{4,7},{5,4},{6,5},{7,6},{8,11},{9,8},{10,9... | collective-permute-start | bytes 1007624 | tf_op jit(solution)/shard_map/ppermute | solution.py:602
  73.8 4.5 %collective-permute-start.9 = (f32[136,128]{1,0:T(8,128)S(1)}, f32[136,128]{1,0:T(8,128)S(1)}, u32[]{:S(2)}, u32[]{:S(2)}) collective-permute-start(f32[136,128]{1,0:T(8,128)S(1)} %get-tuple-element.41), channel_id=1, source_target_pairs={{0,32},{4,36},{8,40},{12,44},{16,48},{20,52},{24,56},{28,60},{32,0... | collective-permute-start | bytes 208904 | tf_op jit(solution)/shard_map/ppermute | solution.py:593
  78.3 0.3 collective-permute-start.10
  78.7 4.7 %collective-permute-done.9.rest_3_ = f32[136,128]{1,0:T(8,128)S(1)} collective-permute-done((f32[136,128]{1,0:T(8,128)S(1)}, f32[136,128]{1,0:T(8,128)S(1)}, u32[]{:S(2)}, u32[]{:S(2)}) %collective-permute-start.9) | collective-permute-done | bytes 69664 | tf_op jit(solution)/shard_map/ppermute | solution.py:593
  83.3 3.6 %collective-permute-start.11 = (f32[136,128]{1,0:T(8,128)S(1)}, f32[136,128]{1,0:T(8,128)S(1)}, u32[]{:S(2)}, u32[]{:S(2)}) collective-permute-start(f32[136,128]{1,0:T(8,128)S(1)} %get-tuple-element.45), channel_id=1, source_target_pairs={{0,48},{4,52},{8,56},{12,60},{16,0},{20,4},{24,8},{28,12},{32,16},... | collective-permute-start | bytes 208904 | tf_op jit(solution)/shard_map/ppermute | solution.py:593
  86.9 2.9 %couple.1 = bf16[2,128,16,128]{3,2,1,0:T(8,128)(2,1)} custom-call(bf16[2,512,512]{2,1,0:T(8,128)(2,1)S(1)} %get-tuple-element.26.high_ref, bf16[2,512,512]{2,1,0:T(8,128)(2,1)S(1)} %get-tuple-element.27.low_ref, f32[2,4,128,128]{3,2,1,0:T(8,128)S(1)} %get-tuple-element.28.near_ref, bf16[2,512,16,128]{3,2,1,0:T(8,128)(2,1)S(1)} %bitcast.11), custom_call_target="tpu_custom_call" | custom-call | flops 2147483648 | bytes 6291456 | tf_op jit(solution)/shard_map/couple/pallas_call | solution.py:453
  89.9 2.0 %assemble.1 = f32[256,1024]{1,0:T(8,128)} custom-call(s32[2]{0:T(128)S(1)} %pad_add_fusion.where_ref, f32[2,128,128]{2,1,0:T(8,128)S(1)} %get-tuple-element.29.own_ref, f32[136,128]{1,0:T(8,128)S(1)} %get-tuple-element.38.rest_0_, f32[272,128]{1,0:T(8,128)S(1)} %collective-permute-done.7.up_ref.rest_1_, ...), custom_call_target="tpu_custom_call" | custom-call | tf_op jit(solution)/shard_map/assemble/pallas_call | solution.py:564
  (16 shorter events, 0.1 us)
Async XLA Ops:
  0.7 1.0 %copy-start.2 = (f32[1,2,128,384]{3,2,1,0:T(8,128)S(1)}, f32[1,2,128,384]{3,2,1,0:T(8,128)}, u32[]{:S(2)}) copy-start(f32[1,2,128,384]{3,2,1,0:T(8,128)} %param.8) | copy-start | bytes 1179652
  1.7 0.7 copy-start.3
  2.4 26.1 %copy-start = (s32[64,128]{1,0:T(8,128)S(1)}, s32[64,128]{1,0:T(8,128)}, u32[]{:S(2)}) copy-start(s32[64,128]{1,0:T(8,128)} %constant.11.clone.table_ref) | copy-start | bytes 98308
  2.4 26.1 %copy-start.1 = (bf16[1,2,512,16,128]{4,3,2,1,0:T(8,128)(2,1)S(1)}, bf16[1,2,512,16,128]{4,3,2,1,0:T(8,128)(2,1)}, u32[]{:S(2)}) copy-start(bf16[1,2,512,16,128]{4,3,2,1,0:T(8,128)(2,1)} %param.9) | copy-start | bytes 12582916
  2.4 26.2 %copy-start.4 = (s32[1,2,16]{2,1,0:T(2,128)S(1)}, s32[1,2,16]{2,1,0:T(2,128)}, u32[]{:S(2)}) copy-start(s32[1,2,16]{2,1,0:T(2,128)} %param.10) | copy-start | bytes 388
  36.6 7.4 %collective-permute-start = (f32[200,128]{1,0:T(8,128)S(1)}, f32[200,128]{1,0:T(8,128)S(1)}, u32[]{:S(2)}, u32[]{:S(2)}) collective-permute-start(f32[200,128]{1,0:T(8,128)S(1)} %get-tuple-element.31), channel_id=1, source_target_pairs={{0,4},{4,0},{8,12},{12,8},{16,20},{20,16},{24,28},{28,24},{32,36},... | collective-permute-start | bytes 307208 | tf_op jit(solution)/shard_map/ppermute | solution.py:593
  36.7 5.6 %collective-permute-start.2 = (f32[136,128]{1,0:T(8,128)S(1)}, f32[136,128]{1,0:T(8,128)S(1)}, u32[]{:S(2)}, u32[]{:S(2)}) collective-permute-start(f32[136,128]{1,0:T(8,128)S(1)} %get-tuple-element.33), channel_id=1, source_target_pairs={{0,68},{4,64},{8,76},{12,72},{16,84},{20,80},{24,92},{28,88},{32,1... | collective-permute-start | bytes 208904 | tf_op jit(solution)/shard_map/ppermute | solution.py:593
  38.4 16.1 %collective-permute-start.1 = (f32[264,128]{1,0:T(8,128)S(1)}, f32[264,128]{1,0:T(8,128)S(1)}, u32[]{:S(2)}, u32[]{:S(2)}) collective-permute-start(f32[264,128]{1,0:T(8,128)S(1)} %get-tuple-element.32), channel_id=1, source_target_pairs={{0,64},{4,68},{8,72},{12,76},{16,80},{20,84},{24,88},{28,92},{32,9... | collective-permute-start | bytes 405512 | tf_op jit(solution)/shard_map/ppermute | solution.py:593
  39.7 14.8 %collective-permute-start.3 = (f32[264,128]{1,0:T(8,128)S(1)}, f32[264,128]{1,0:T(8,128)S(1)}, u32[]{:S(2)}, u32[]{:S(2)}) collective-permute-start(f32[264,128]{1,0:T(8,128)S(1)} %get-tuple-element.34), channel_id=1, source_target_pairs={{0,128},{4,132},{8,136},{12,140},{16,144},{20,148},{24,152},{28,15... | collective-permute-start | bytes 405512 | tf_op jit(solution)/shard_map/ppermute | solution.py:593
  41.1 13.4 %collective-permute-start.4 = (f32[264,128]{1,0:T(8,128)S(1)}, f32[264,128]{1,0:T(8,128)S(1)}, u32[]{:S(2)}, u32[]{:S(2)}) collective-permute-start(f32[264,128]{1,0:T(8,128)S(1)} %get-tuple-element.35), channel_id=1, source_target_pairs={{0,132},{4,128},{8,140},{12,136},{16,148},{20,144},{24,156},{28,15... | collective-permute-start | bytes 405512 | tf_op jit(solution)/shard_map/ppermute | solution.py:593
  42.4 12.1 %collective-permute-start.5 = (f32[264,128]{1,0:T(8,128)S(1)}, f32[264,128]{1,0:T(8,128)S(1)}, u32[]{:S(2)}, u32[]{:S(2)}) collective-permute-start(f32[264,128]{1,0:T(8,128)S(1)} %get-tuple-element.36), channel_id=1, source_target_pairs={{0,192},{4,196},{8,200},{12,204},{16,208},{20,212},{24,216},{28,22... | collective-permute-start | bytes 405512 | tf_op jit(solution)/shard_map/ppermute | solution.py:593
  44.1 10.4 %collective-permute-start.6 = (f32[200,128]{1,0:T(8,128)S(1)}, f32[200,128]{1,0:T(8,128)S(1)}, u32[]{:S(2)}, u32[]{:S(2)}) collective-permute-start(f32[200,128]{1,0:T(8,128)S(1)} %get-tuple-element.37), channel_id=1, source_target_pairs={{0,196},{4,192},{8,204},{12,200},{16,212},{20,208},{24,220},{28,21... | collective-permute-start | bytes 307208 | tf_op jit(solution)/shard_map/ppermute | solution.py:593
  56.1 17.7 %collective-permute-start.7 = (f32[272,128]{1,0:T(8,128)S(1)}, f32[272,128]{1,0:T(8,128)S(1)}, u32[]{:S(2)}, u32[]{:S(2)}) collective-permute-start(f32[272,128]{1,0:T(8,128)S(1)} %get-tuple-element.39), channel_id=1, source_target_pairs={{0,8},{4,12},{8,16},{12,20},{16,24},{20,28},{24,32},{28,36},{32,40... | collective-permute-start | bytes 417800 | tf_op jit(solution)/shard_map/ppermute | solution.py:593
  58.1 20.2 %collective-permute-start.8 = (f32[272,128]{1,0:T(8,128)S(1)}, f32[272,128]{1,0:T(8,128)S(1)}, u32[]{:S(2)}, u32[]{:S(2)}) collective-permute-start(f32[272,128]{1,0:T(8,128)S(1)} %get-tuple-element.40), channel_id=1, source_target_pairs={{0,56},{4,60},{8,0},{12,4},{16,8},{20,12},{24,16},{28,20},{32,24},... | collective-permute-start | bytes 417800 | tf_op jit(solution)/shard_map/ppermute | solution.py:593
  67.8 22.0 %collective-permute-start.12 = (f32[2,328,128]{2,1,0:T(8,128)S(1)}, f32[2,328,128]{2,1,0:T(8,128)S(1)}, u32[]{:S(2)}, u32[]{:S(2)}) collective-permute-start(f32[2,328,128]{2,1,0:T(8,128)S(1)} %get-tuple-element.47.rest_7_), channel_id=1, source_target_pairs={{0,1},{1,2},{2,3},{3,0},{4,5},{5,6},{6,7},{7,4},{8,9},{9,10},{10,1... | collective-permute-start | bytes 1007624 | tf_op jit(solution)/shard_map/ppermute | solution.py:602
  69.6 20.2 %collective-permute-start.13 = (f32[2,328,128]{2,1,0:T(8,128)S(1)}, f32[2,328,128]{2,1,0:T(8,128)S(1)}, u32[]{:S(2)}, u32[]{:S(2)}) collective-permute-start(f32[2,328,128]{2,1,0:T(8,128)S(1)} %get-tuple-element.48.rest_8_), channel_id=1, source_target_pairs={{0,2},{1,3},{2,0},{3,1},{4,6},{5,7},{6,4},{7,5},{8,10},{9,11},{10,... | collective-permute-start | bytes 1007624 | tf_op jit(solution)/shard_map/ppermute | solution.py:602
  72.4 17.5 %collective-permute-start.14 = (f32[2,328,128]{2,1,0:T(8,128)S(1)}, f32[2,328,128]{2,1,0:T(8,128)S(1)}, u32[]{:S(2)}, u32[]{:S(2)}) collective-permute-start(f32[2,328,128]{2,1,0:T(8,128)S(1)} %get-tuple-element.49.rest_9_), channel_id=1, source_target_pairs={{0,3},{1,0},{2,1},{3,2},{4,7},{5,4},{6,5},{7,6},{8,11},{9,8},{10,9... | collective-permute-start | bytes 1007624 | tf_op jit(solution)/shard_map/ppermute | solution.py:602
  73.8 9.5 %collective-permute-start.9 = (f32[136,128]{1,0:T(8,128)S(1)}, f32[136,128]{1,0:T(8,128)S(1)}, u32[]{:S(2)}, u32[]{:S(2)}) collective-permute-start(f32[136,128]{1,0:T(8,128)S(1)} %get-tuple-element.41), channel_id=1, source_target_pairs={{0,32},{4,36},{8,40},{12,44},{16,48},{20,52},{24,56},{28,60},{32,0... | collective-permute-start | bytes 208904 | tf_op jit(solution)/shard_map/ppermute | solution.py:593
  78.3 11.5 %collective-permute-start.10 = (f32[136,128]{1,0:T(8,128)S(1)}, f32[136,128]{1,0:T(8,128)S(1)}, u32[]{:S(2)}, u32[]{:S(2)}) collective-permute-start(f32[136,128]{1,0:T(8,128)S(1)} %get-tuple-element.44), channel_id=1, source_target_pairs={{0,16},{4,20},{8,24},{12,28},{16,32},{20,36},{24,40},{28,44},{32,4... | collective-permute-start | bytes 208904 | tf_op jit(solution)/shard_map/ppermute | solution.py:593
  83.3 6.5 %collective-permute-start.11 = (f32[136,128]{1,0:T(8,128)S(1)}, f32[136,128]{1,0:T(8,128)S(1)}, u32[]{:S(2)}, u32[]{:S(2)}) collective-permute-start(f32[136,128]{1,0:T(8,128)S(1)} %get-tuple-element.45), channel_id=1, source_target_pairs={{0,48},{4,52},{8,56},{12,60},{16,0},{20,4},{24,8},{28,12},{32,16},... | collective-permute-start | bytes 208904 | tf_op jit(solution)/shard_map/ppermute | solution.py:593

commit v2 on v1

--- a/solution.py
+++ b/solution.py
@@ -34,6 +34,12 @@
     rest = x - hi.astype(F32)
     mid = rest.astype(BF16)
     return hi, mid, (rest - mid.astype(F32)).astype(BF16)
+
+
+def dot3(a, b, dims=NN):
+    ah, al = split2(a)
+    bh, bl = split2(b)
+    return dot_bf16(ah, bh, dims) + (dot_bf16(ah, bl, dims) + dot_bf16(al, bh, dims))
 
 
 def iota(shape, dim):
@@ -211,7 +217,7 @@
         high_ref[b, :red] = grid_high
         low_ref[b, :red] = grid_low
         place_s = one_hot_rows(orders_ref[b : b + 1, :], skel, dof)
-        last_high, last_low = split2(place_s - dot_high(solved_t, aug[b, :, :dof]))
+        last_high, last_low = split2(place_s - dot3(solved_t, aug[b, :, :dof]))
         high_ref[b, red:] = last_high
         low_ref[b, red:] = last_low
 
@@ -377,57 +383,50 @@
     )(ids, where, table, high, low, w)
 
 
-def near_kernel(ids_ref, where_ref, high_ref, low_ref, w_ref, *rest):
-    near_ref, sib_outs, sib = rest[0], rest[1:-1], rest[-1]
-    box = pl.program_id(0)
+def near_kernel(ids_ref, where_ref, high_ref, low_ref, w_ref, near_ref, *sib_outs):
     this_sib = where_ref[1]
     red = high_ref.shape[1] - w_ref.shape[3]
-
-    @pl.when(box == 0)
-    def _():
-        sib[...] = jnp.zeros_like(sib)
-
-    by_slot = jnp.swapaxes(w_ref[0, :, :8], 0, 1)
-    for first in range(0, NSIB, 2):
-        pair = jnp.concatenate([by_slot[first], by_slot[first + 1]], axis=1)
-        product = dot_bf16(high_ref[0], pair) + dot_bf16(low_ref[0], pair)
-        both = gram(product[:red].T)
+    count = w_ref.shape[0]
+    sib = sib_outs[-1]
+    sib[...] = jnp.zeros_like(sib)
+
+    found = []
+    for box in range(count):
+        by_slot = jnp.swapaxes(w_ref[box, :, :8], 0, 1)
+        for first in range(0, NSIB, 2):
+            pair = jnp.concatenate([by_slot[first], by_slot[first + 1]], axis=1)
+            product = dot_bf16(high_ref[box], pair) + dot_bf16(low_ref[box], pair)
+            found.append((box, first, product[red:], gram(product[:red].T)))
+    for box, first, last, both in found:
         for s in range(2):
             part = slice(128 * s, 128 * (s + 1))
-            coupled = product[red:, part]
-            near_ref[0, first + s] = coupled
+            coupled = last[:, part]
+            near_ref[box, first + s] = coupled
             other = ids_ref[box, first + s]
             child = other & 1
             body, tail = pack_symmetric(both[part, part], child.astype(F32))
             place = ((((other >> 1) & 3) - this_sib) & 3) * 2 + child
-            rows = pl.ds(pl.multiple_of(box * 128, 128), 128)
+            rows = slice(128 * box, 128 * (box + 1))
             sib[place, rows, :] = coupled
             sib[place, 256:320, :] = sib[place, 256:320, :] + body
             sib[place, 320:321, :] = sib[place, 320:321, :] + tail
 
-    @pl.when(box == pl.num_programs(0) - 1)
-    def _():
-        for i, out in enumerate(sib_outs):
-            out[...] = sib[2 * i : 2 * i + 2]
+    for i, out in enumerate(sib_outs[:-1]):
+        out[...] = sib[2 * i : 2 * i + 2]
 
 
 def near_updates(ids, where, high, low, w, interpret=False):
-    count, dof, slots, skel = w.shape
-    by_box = lambda shape: pl.BlockSpec((1,) + shape, lambda b, *_: (b,) + (0,) * len(shape))
+    count, _, _, skel = w.shape
     return pl.pallas_call(
         near_kernel,
         out_shape=(
             [jax.ShapeDtypeStruct((count, NSIB, skel, skel), F32)]
             + [jax.ShapeDtypeStruct((2, 328, 128), F32)] * 4
         ),
-        grid_spec=pltpu.PrefetchScalarGridSpec(
-            num_scalar_prefetch=2,
-            grid=(count,),
-            in_specs=[by_box((dof, dof)), by_box((dof, dof)), by_box((dof, slots, skel))],
-            out_specs=[by_box((NSIB, skel, skel))]
-            + [pl.BlockSpec((2, 328, 128), lambda b, *_: (0, 0, 0))] * 4,
-            scratch_shapes=[pltpu.VMEM((8, 328, 128), F32)],
-        ),
+        in_specs=[pl.BlockSpec(memory_space=pltpu.SMEM)] * 2
+        + [pl.BlockSpec(memory_space=pltpu.VMEM)] * 3,
+        out_specs=[pl.BlockSpec(memory_space=pltpu.VMEM)] * 5,
+        scratch_shapes=[pltpu.VMEM((8, 328, 128), F32)],
         compiler_params=pltpu.CompilerParams(vmem_limit_bytes=28 << 20),
         cost_estimate=pl.CostEstimate(flops=3 << 30, bytes_accessed=8 << 20, transcendentals=0),
         interpret=interpret,

time: 92 us -> 90.4 us (0.983)
  starting transfers between devices: 29 us -> 27.2 us
    ppermute x12, starting transfers between devices: 23 us -> 21.5 us  [shifted(): return lax.ppermute(block, 'box', moves)]
  transfers between devices with their start and end apart: 15 -> 15, of which waited for: 2 -> 3; matrix products, arithmetic and copies ran while one was open for 0% -> 0% of each run, Pallas kernels for 9% -> 9%
where the time goes in v2:
time: 90.4 us; the launch traced here: 90.2 us
  Pallas kernels  45.9 us (51%)
  starting transfers between devices  27.2 us (30%)
  waiting for transfers between devices  14.6 us (16%)
  local copies, waits for them, and re-layouts  1.69 us (2%)
    pallas_call x1, Pallas kernels, factor(): pl.pallas_call(factor_kernel, out_shape=(jax.ShapeDtypeStruct((count, dof...  25.9 us
    ppermute x12, starting transfers between devices, shifted(): return lax.ppermute(block, 'box', moves)  21.5 us
    ppermute x12, waiting for transfers between devices, shifted(): return lax.ppermute(block, 'box', moves)  14.6 us
    pallas_call x1, Pallas kernels, far_updates(): pl.pallas_call(functools.partial(far_kernel, caps=caps, starts=starts, bo...  8.08 us
    ppermute x3, starting transfers between devices, on_device(): sib_got.append(lax.ppermute(kept[s], 'sib', moves))  5.73 us
    pallas_call x1, Pallas kernels, near_updates(): pl.pallas_call(near_kernel, out_shape=[jax.ShapeDtypeStruct((count, NSIB,...  5.4 us
    pallas_call x1, Pallas kernels, couple(): pl.pallas_call(couple_kernel, out_shape=jax.ShapeDtypeStruct((count, skel...  2.94 us
    pallas_call x1, Pallas kernels, assemble(): pl.pallas_call(assemble_kernel, out_shape=jax.ShapeDtypeStruct((256, 1024...  2 us
  transfers between devices with their start and end apart: 15, of which 3 were waited for; matrix products, arithmetic and copies ran while one was open for 0% of the time, Pallas kernels for 9%

profile of v2, /device:TPU:8, one launch (start us, length us, event | category | flops | bytes accessed | tf_op | source)
XLA Modules:
  0.0 90.2 jit_solution(4407772212809867677)
XLA Ops:
  0.6 0.1 pad_add_fusion.where_ref
  0.7 1.0 %copy-done.2 = f32[1,2,128,384]{3,2,1,0:T(8,128)S(1)} copy-done((f32[1,2,128,384]{3,2,1,0:T(8,128)S(1)}, f32[1,2,128,384]{3,2,1,0:T(8,128)}, u32[]{:S(2)}) %copy-start.2) | copy-done | bytes 393240
  1.7 0.7 copy-done.3
  2.4 25.9 %factor.1 = (bf16[2,512,512]{2,1,0:T(8,128)(2,1)S(1)}, bf16[2,512,512]{2,1,0:T(8,128)(2,1)S(1)}, f32[2,128,128]{2,1,0:T(8,128)S(1)}) custom-call(f32[2,512,512]{2,1,0:T(8,128)} %bitcast.17, s32[2,512]{1,0:T(2,128)S(1)} %bitcast.13, f32[2,128,384]{2,1,0:T(8,128)S(1)} %bitcast.12), custom_call_target="tpu_custom_call" | custom-call | flops 8589934592 | bytes 6291456 | tf_op jit(solution)/shard_map/factor/pallas_call | solution.py:228
  28.3 8.1 %far_updates.1 = (f32[264,128]{1,0:T(8,128)S(1)}, f32[200,128]{1,0:T(8,128)S(1)}, f32[264,128]{1,0:T(8,128)S(1)}, f32[136,128]{1,0:T(8,128)S(1)}, f32[264,128]{1...) custom-call(s32[2,16]{1,0:T(2,128)S(1)} %bitcast.14, ...), custom_call_target="tpu_custom_call" | custom-call | flops 6442450944 | bytes 8388608 | tf_op jit(solution)/shard_map/far_updates/pallas_call | solution.py:365
  36.4 0.1 collective-permute-start
  36.5 1.7 %collective-permute-start.2 = (f32[136,128]{1,0:T(8,128)S(1)}, f32[136,128]{1,0:T(8,128)S(1)}, u32[]{:S(2)}, u32[]{:S(2)}) collective-permute-start(f32[136,128]{1,0:T(8,128)S(1)} %get-tuple-element.33), channel_id=1, source_target_pairs={{0,68},{4,64},{8,76},{12,72},{16,84},{20,80},{24,92},{28,88},{32,1... | collective-permute-start | bytes 208904 | tf_op jit(solution)/shard_map/ppermute | solution.py:592
  38.2 1.3 %collective-permute-start.1 = (f32[264,128]{1,0:T(8,128)S(1)}, f32[264,128]{1,0:T(8,128)S(1)}, u32[]{:S(2)}, u32[]{:S(2)}) collective-permute-start(f32[264,128]{1,0:T(8,128)S(1)} %get-tuple-element.32), channel_id=1, source_target_pairs={{0,64},{4,68},{8,72},{12,76},{16,80},{20,84},{24,88},{28,92},{32,9... | collective-permute-start | bytes 405512 | tf_op jit(solution)/shard_map/ppermute | solution.py:592
  39.5 1.4 %collective-permute-start.3 = (f32[264,128]{1,0:T(8,128)S(1)}, f32[264,128]{1,0:T(8,128)S(1)}, u32[]{:S(2)}, u32[]{:S(2)}) collective-permute-start(f32[264,128]{1,0:T(8,128)S(1)} %get-tuple-element.34), channel_id=1, source_target_pairs={{0,128},{4,132},{8,136},{12,140},{16,144},{20,148},{24,152},{28,15... | collective-permute-start | bytes 405512 | tf_op jit(solution)/shard_map/ppermute | solution.py:592
  40.9 1.2 %collective-permute-start.4 = (f32[264,128]{1,0:T(8,128)S(1)}, f32[264,128]{1,0:T(8,128)S(1)}, u32[]{:S(2)}, u32[]{:S(2)}) collective-permute-start(f32[264,128]{1,0:T(8,128)S(1)} %get-tuple-element.35), channel_id=1, source_target_pairs={{0,132},{4,128},{8,140},{12,136},{16,148},{20,144},{24,156},{28,15... | collective-permute-start | bytes 405512 | tf_op jit(solution)/shard_map/ppermute | solution.py:592
  42.1 0.0 collective-permute-done.2.rest_3_
  42.1 1.7 %collective-permute-start.5 = (f32[264,128]{1,0:T(8,128)S(1)}, f32[264,128]{1,0:T(8,128)S(1)}, u32[]{:S(2)}, u32[]{:S(2)}) collective-permute-start(f32[264,128]{1,0:T(8,128)S(1)} %get-tuple-element.36), channel_id=1, source_target_pairs={{0,192},{4,196},{8,200},{12,204},{16,208},{20,212},{24,216},{28,22... | collective-permute-start | bytes 405512 | tf_op jit(solution)/shard_map/ppermute | solution.py:592
  43.8 0.0 collective-permute-done.rest_1_
  43.8 1.2 %collective-permute-start.6 = (f32[200,128]{1,0:T(8,128)S(1)}, f32[200,128]{1,0:T(8,128)S(1)}, u32[]{:S(2)}, u32[]{:S(2)}) collective-permute-start(f32[200,128]{1,0:T(8,128)S(1)} %get-tuple-element.37), channel_id=1, source_target_pairs={{0,196},{4,192},{8,204},{12,200},{16,212},{20,208},{24,220},{28,21... | collective-permute-start | bytes 307208 | tf_op jit(solution)/shard_map/ppermute | solution.py:592
  45.1 9.2 %collective-permute-done.6.rest_7_ = f32[200,128]{1,0:T(8,128)S(1)} collective-permute-done((f32[200,128]{1,0:T(8,128)S(1)}, f32[200,128]{1,0:T(8,128)S(1)}, u32[]{:S(2)}, u32[]{:S(2)}) %collective-permute-start.6) | collective-permute-done | bytes 102432 | tf_op jit(solution)/shard_map/ppermute | solution.py:592
  54.3 0.0 collective-permute-done.3.rest_4_
  54.3 0.0 collective-permute-done.4.rest_5_
  54.3 0.0 collective-permute-done.5.rest_6_
  54.3 1.5 %route.1 = (f32[136,128]{1,0:T(8,128)S(1)}, f32[272,128]{1,0:T(8,128)S(1)}, f32[272,128]{1,0:T(8,128)S(1)}, f32[136,128]{1,0:T(8,128)S(1)}, f32[136,128]{1,0:T(8,128)S(1)}, /*index=5*/f32[136,128]{1,0:T(8,128)S(1)}) custom-call(s32[2]{0:T(128)S(1)} %pad_add_fusion.where_ref, s32[64,128]{1,0:T(8,128)S(1)} %copy-done, ...), custom_call_target="tpu_custom_call" | custom-call | flops 4194304 | bytes 2097152 | tf_op jit(solution)/shard_map/route/pallas_call | solution.py:493
  55.8 2.0 %collective-permute-start.7 = (f32[272,128]{1,0:T(8,128)S(1)}, f32[272,128]{1,0:T(8,128)S(1)}, u32[]{:S(2)}, u32[]{:S(2)}) collective-permute-start(f32[272,128]{1,0:T(8,128)S(1)} %get-tuple-element.39), channel_id=1, source_target_pairs={{0,8},{4,12},{8,16},{12,20},{16,24},{20,28},{24,32},{28,36},{32,40... | collective-permute-start | bytes 417800 | tf_op jit(solution)/shard_map/ppermute | solution.py:592
  57.8 4.3 %collective-permute-start.8 = (f32[272,128]{1,0:T(8,128)S(1)}, f32[272,128]{1,0:T(8,128)S(1)}, u32[]{:S(2)}, u32[]{:S(2)}) collective-permute-start(f32[272,128]{1,0:T(8,128)S(1)} %get-tuple-element.40), channel_id=1, source_target_pairs={{0,56},{4,60},{8,0},{12,4},{16,8},{20,12},{24,16},{28,20},{32,24},... | collective-permute-start | bytes 417800 | tf_op jit(solution)/shard_map/ppermute | solution.py:592
  62.1 5.4 %near_updates.1 = (f32[2,4,128,128]{3,2,1,0:T(8,128)S(1)}, f32[2,328,128]{2,1,0:T(8,128)S(1)}, f32[2,328,128]{2,1,0:T(8,128)S(1)}, f32[2,328,128]{2,1,0:T(8,128)S(1)}, f32[2,328,128]{2,1,0:T(8,128)S(1)}) custom-call(s32[2,16]{1,0:T(2,128)S(1)} %bitcast.15, s32[2]{0:T(128)S(1)} %pad_add_fusion.where_ref, bf16[2,512,512]{2,1,0:T(8,128)(2,1)S(1)} %get-tuple-element.26.high_ref, ...), custom_call_target="tpu_custom_call" | custom-call | flops 3221225472 | bytes 8388608 | tf_op jit(solution)/shard_map/near_updates/pallas_call | solution.py:420
  67.5 1.6 %collective-permute-start.12 = (f32[2,328,128]{2,1,0:T(8,128)S(1)}, f32[2,328,128]{2,1,0:T(8,128)S(1)}, u32[]{:S(2)}, u32[]{:S(2)}) collective-permute-start(f32[2,328,128]{2,1,0:T(8,128)S(1)} %get-tuple-element.47.rest_7_), channel_id=1, source_target_pairs={{0,1},{1,2},{2,3},{3,0},{4,5},{5,6},{6,7},{7,4},{8,9},{9,10},{10,1... | collective-permute-start | bytes 1007624 | tf_op jit(solution)/shard_map/ppermute | solution.py:601
  69.1 2.7 %collective-permute-start.13 = (f32[2,328,128]{2,1,0:T(8,128)S(1)}, f32[2,328,128]{2,1,0:T(8,128)S(1)}, u32[]{:S(2)}, u32[]{:S(2)}) collective-permute-start(f32[2,328,128]{2,1,0:T(8,128)S(1)} %get-tuple-element.48.rest_8_), channel_id=1, source_target_pairs={{0,2},{1,3},{2,0},{3,1},{4,6},{5,7},{6,4},{7,5},{8,10},{9,11},{10,... | collective-permute-start | bytes 1007624 | tf_op jit(solution)/shard_map/ppermute | solution.py:601
  71.8 1.4 %collective-permute-start.14 = (f32[2,328,128]{2,1,0:T(8,128)S(1)}, f32[2,328,128]{2,1,0:T(8,128)S(1)}, u32[]{:S(2)}, u32[]{:S(2)}) collective-permute-start(f32[2,328,128]{2,1,0:T(8,128)S(1)} %get-tuple-element.49.rest_9_), channel_id=1, source_target_pairs={{0,3},{1,0},{2,1},{3,2},{4,7},{5,4},{6,5},{7,6},{8,11},{9,8},{10,9... | collective-permute-start | bytes 1007624 | tf_op jit(solution)/shard_map/ppermute | solution.py:601
  73.2 4.2 %collective-permute-start.9 = (f32[136,128]{1,0:T(8,128)S(1)}, f32[136,128]{1,0:T(8,128)S(1)}, u32[]{:S(2)}, u32[]{:S(2)}) collective-permute-start(f32[136,128]{1,0:T(8,128)S(1)} %get-tuple-element.41), channel_id=1, source_target_pairs={{0,32},{4,36},{8,40},{12,44},{16,48},{20,52},{24,56},{28,60},{32,0... | collective-permute-start | bytes 208904 | tf_op jit(solution)/shard_map/ppermute | solution.py:592
  77.5 0.3 collective-permute-start.10
  77.8 5.2 %collective-permute-done.9.rest_3_ = f32[136,128]{1,0:T(8,128)S(1)} collective-permute-done((f32[136,128]{1,0:T(8,128)S(1)}, f32[136,128]{1,0:T(8,128)S(1)}, u32[]{:S(2)}, u32[]{:S(2)}) %collective-permute-start.9) | collective-permute-done | bytes 69664 | tf_op jit(solution)/shard_map/ppermute | solution.py:592
  83.0 2.0 %collective-permute-start.11 = (f32[136,128]{1,0:T(8,128)S(1)}, f32[136,128]{1,0:T(8,128)S(1)}, u32[]{:S(2)}, u32[]{:S(2)}) collective-permute-start(f32[136,128]{1,0:T(8,128)S(1)} %get-tuple-element.45), channel_id=1, source_target_pairs={{0,48},{4,52},{8,56},{12,60},{16,0},{20,4},{24,8},{28,12},{32,16},... | collective-permute-start | bytes 208904 | tf_op jit(solution)/shard_map/ppermute | solution.py:592
  85.1 2.9 %couple.1 = bf16[2,128,16,128]{3,2,1,0:T(8,128)(2,1)} custom-call(bf16[2,512,512]{2,1,0:T(8,128)(2,1)S(1)} %get-tuple-element.26.high_ref, bf16[2,512,512]{2,1,0:T(8,128)(2,1)S(1)} %get-tuple-element.27.low_ref, f32[2,4,128,128]{3,2,1,0:T(8,128)S(1)} %get-tuple-element.28.near_ref, bf16[2,512,16,128]{3,2,1,0:T(8,128)(2,1)S(1)} %bitcast.11), custom_call_target="tpu_custom_call" | custom-call | flops 2147483648 | bytes 6291456 | tf_op jit(solution)/shard_map/couple/pallas_call | solution.py:452
  88.0 0.2 collective-permute-done.11.rest_5_
  88.2 2.0 %assemble.1 = f32[256,1024]{1,0:T(8,128)} custom-call(s32[2]{0:T(128)S(1)} %pad_add_fusion.where_ref, f32[2,128,128]{2,1,0:T(8,128)S(1)} %get-tuple-element.29.own_ref, f32[136,128]{1,0:T(8,128)S(1)} %get-tuple-element.38.rest_0_, f32[272,128]{1,0:T(8,128)S(1)} %collective-permute-done.7.up_ref.rest_1_, ...), custom_call_target="tpu_custom_call" | custom-call | tf_op jit(solution)/shard_map/assemble/pallas_call | solution.py:563
  (16 shorter events, 0.1 us)
Async XLA Ops:
  0.7 1.0 %copy-start.2 = (f32[1,2,128,384]{3,2,1,0:T(8,128)S(1)}, f32[1,2,128,384]{3,2,1,0:T(8,128)}, u32[]{:S(2)}) copy-start(f32[1,2,128,384]{3,2,1,0:T(8,128)} %param.8) | copy-start | bytes 1179652
  1.7 0.7 copy-start.3
  2.4 25.9 %copy-start = (s32[64,128]{1,0:T(8,128)S(1)}, s32[64,128]{1,0:T(8,128)}, u32[]{:S(2)}) copy-start(s32[64,128]{1,0:T(8,128)} %constant.11.clone.table_ref) | copy-start | bytes 98308
  2.4 25.9 %copy-start.1 = (bf16[1,2,512,16,128]{4,3,2,1,0:T(8,128)(2,1)S(1)}, bf16[1,2,512,16,128]{4,3,2,1,0:T(8,128)(2,1)}, u32[]{:S(2)}) copy-start(bf16[1,2,512,16,128]{4,3,2,1,0:T(8,128)(2,1)} %param.9) | copy-start | bytes 12582916
  2.4 25.9 %copy-start.4 = (s32[1,2,16]{2,1,0:T(2,128)S(1)}, s32[1,2,16]{2,1,0:T(2,128)}, u32[]{:S(2)}) copy-start(s32[1,2,16]{2,1,0:T(2,128)} %param.10) | copy-start | bytes 388
  36.4 7.4 %collective-permute-start = (f32[200,128]{1,0:T(8,128)S(1)}, f32[200,128]{1,0:T(8,128)S(1)}, u32[]{:S(2)}, u32[]{:S(2)}) collective-permute-start(f32[200,128]{1,0:T(8,128)S(1)} %get-tuple-element.31), channel_id=1, source_target_pairs={{0,4},{4,0},{8,12},{12,8},{16,20},{20,16},{24,28},{28,24},{32,36},... | collective-permute-start | bytes 307208 | tf_op jit(solution)/shard_map/ppermute | solution.py:592
  36.5 5.6 %collective-permute-start.2 = (f32[136,128]{1,0:T(8,128)S(1)}, f32[136,128]{1,0:T(8,128)S(1)}, u32[]{:S(2)}, u32[]{:S(2)}) collective-permute-start(f32[136,128]{1,0:T(8,128)S(1)} %get-tuple-element.33), channel_id=1, source_target_pairs={{0,68},{4,64},{8,76},{12,72},{16,84},{20,80},{24,92},{28,88},{32,1... | collective-permute-start | bytes 208904 | tf_op jit(solution)/shard_map/ppermute | solution.py:592
  38.2 16.1 %collective-permute-start.1 = (f32[264,128]{1,0:T(8,128)S(1)}, f32[264,128]{1,0:T(8,128)S(1)}, u32[]{:S(2)}, u32[]{:S(2)}) collective-permute-start(f32[264,128]{1,0:T(8,128)S(1)} %get-tuple-element.32), channel_id=1, source_target_pairs={{0,64},{4,68},{8,72},{12,76},{16,80},{20,84},{24,88},{28,92},{32,9... | collective-permute-start | bytes 405512 | tf_op jit(solution)/shard_map/ppermute | solution.py:592
  39.5 14.8 %collective-permute-start.3 = (f32[264,128]{1,0:T(8,128)S(1)}, f32[264,128]{1,0:T(8,128)S(1)}, u32[]{:S(2)}, u32[]{:S(2)}) collective-permute-start(f32[264,128]{1,0:T(8,128)S(1)} %get-tuple-element.34), channel_id=1, source_target_pairs={{0,128},{4,132},{8,136},{12,140},{16,144},{20,148},{24,152},{28,15... | collective-permute-start | bytes 405512 | tf_op jit(solution)/shard_map/ppermute | solution.py:592
  40.9 13.4 %collective-permute-start.4 = (f32[264,128]{1,0:T(8,128)S(1)}, f32[264,128]{1,0:T(8,128)S(1)}, u32[]{:S(2)}, u32[]{:S(2)}) collective-permute-start(f32[264,128]{1,0:T(8,128)S(1)} %get-tuple-element.35), channel_id=1, source_target_pairs={{0,132},{4,128},{8,140},{12,136},{16,148},{20,144},{24,156},{28,15... | collective-permute-start | bytes 405512 | tf_op jit(solution)/shard_map/ppermute | solution.py:592
  42.1 12.1 %collective-permute-start.5 = (f32[264,128]{1,0:T(8,128)S(1)}, f32[264,128]{1,0:T(8,128)S(1)}, u32[]{:S(2)}, u32[]{:S(2)}) collective-permute-start(f32[264,128]{1,0:T(8,128)S(1)} %get-tuple-element.36), channel_id=1, source_target_pairs={{0,192},{4,196},{8,200},{12,204},{16,208},{20,212},{24,216},{28,22... | collective-permute-start | bytes 405512 | tf_op jit(solution)/shard_map/ppermute | solution.py:592
  43.8 10.4 %collective-permute-start.6 = (f32[200,128]{1,0:T(8,128)S(1)}, f32[200,128]{1,0:T(8,128)S(1)}, u32[]{:S(2)}, u32[]{:S(2)}) collective-permute-start(f32[200,128]{1,0:T(8,128)S(1)} %get-tuple-element.37), channel_id=1, source_target_pairs={{0,196},{4,192},{8,204},{12,200},{16,212},{20,208},{24,220},{28,21... | collective-permute-start | bytes 307208 | tf_op jit(solution)/shard_map/ppermute | solution.py:592
  55.8 17.4 %collective-permute-start.7 = (f32[272,128]{1,0:T(8,128)S(1)}, f32[272,128]{1,0:T(8,128)S(1)}, u32[]{:S(2)}, u32[]{:S(2)}) collective-permute-start(f32[272,128]{1,0:T(8,128)S(1)} %get-tuple-element.39), channel_id=1, source_target_pairs={{0,8},{4,12},{8,16},{12,20},{16,24},{20,28},{24,32},{28,36},{32,40... | collective-permute-start | bytes 417800 | tf_op jit(solution)/shard_map/ppermute | solution.py:592
  57.8 19.7 %collective-permute-start.8 = (f32[272,128]{1,0:T(8,128)S(1)}, f32[272,128]{1,0:T(8,128)S(1)}, u32[]{:S(2)}, u32[]{:S(2)}) collective-permute-start(f32[272,128]{1,0:T(8,128)S(1)} %get-tuple-element.40), channel_id=1, source_target_pairs={{0,56},{4,60},{8,0},{12,4},{16,8},{20,12},{24,16},{28,20},{32,24},... | collective-permute-start | bytes 417800 | tf_op jit(solution)/shard_map/ppermute | solution.py:592
  67.5 20.5 %collective-permute-start.12 = (f32[2,328,128]{2,1,0:T(8,128)S(1)}, f32[2,328,128]{2,1,0:T(8,128)S(1)}, u32[]{:S(2)}, u32[]{:S(2)}) collective-permute-start(f32[2,328,128]{2,1,0:T(8,128)S(1)} %get-tuple-element.47.rest_7_), channel_id=1, source_target_pairs={{0,1},{1,2},{2,3},{3,0},{4,5},{5,6},{6,7},{7,4},{8,9},{9,10},{10,1... | collective-permute-start | bytes 1007624 | tf_op jit(solution)/shard_map/ppermute | solution.py:601
  69.1 18.9 %collective-permute-start.13 = (f32[2,328,128]{2,1,0:T(8,128)S(1)}, f32[2,328,128]{2,1,0:T(8,128)S(1)}, u32[]{:S(2)}, u32[]{:S(2)}) collective-permute-start(f32[2,328,128]{2,1,0:T(8,128)S(1)} %get-tuple-element.48.rest_8_), channel_id=1, source_target_pairs={{0,2},{1,3},{2,0},{3,1},{4,6},{5,7},{6,4},{7,5},{8,10},{9,11},{10,... | collective-permute-start | bytes 1007624 | tf_op jit(solution)/shard_map/ppermute | solution.py:601
  71.8 16.2 %collective-permute-start.14 = (f32[2,328,128]{2,1,0:T(8,128)S(1)}, f32[2,328,128]{2,1,0:T(8,128)S(1)}, u32[]{:S(2)}, u32[]{:S(2)}) collective-permute-start(f32[2,328,128]{2,1,0:T(8,128)S(1)} %get-tuple-element.49.rest_9_), channel_id=1, source_target_pairs={{0,3},{1,0},{2,1},{3,2},{4,7},{5,4},{6,5},{7,6},{8,11},{9,8},{10,9... | collective-permute-start | bytes 1007624 | tf_op jit(solution)/shard_map/ppermute | solution.py:601
  73.2 9.8 %collective-permute-start.9 = (f32[136,128]{1,0:T(8,128)S(1)}, f32[136,128]{1,0:T(8,128)S(1)}, u32[]{:S(2)}, u32[]{:S(2)}) collective-permute-start(f32[136,128]{1,0:T(8,128)S(1)} %get-tuple-element.41), channel_id=1, source_target_pairs={{0,32},{4,36},{8,40},{12,44},{16,48},{20,52},{24,56},{28,60},{32,0... | collective-permute-start | bytes 208904 | tf_op jit(solution)/shard_map/ppermute | solution.py:592
  77.5 10.5 %collective-permute-start.10 = (f32[136,128]{1,0:T(8,128)S(1)}, f32[136,128]{1,0:T(8,128)S(1)}, u32[]{:S(2)}, u32[]{:S(2)}) collective-permute-start(f32[136,128]{1,0:T(8,128)S(1)} %get-tuple-element.44), channel_id=1, source_target_pairs={{0,16},{4,20},{8,24},{12,28},{16,32},{20,36},{24,40},{28,44},{32,4... | collective-permute-start | bytes 208904 | tf_op jit(solution)/shard_map/ppermute | solution.py:592
  83.0 5.2 %collective-permute-start.11 = (f32[136,128]{1,0:T(8,128)S(1)}, f32[136,128]{1,0:T(8,128)S(1)}, u32[]{:S(2)}, u32[]{:S(2)}) collective-permute-start(f32[136,128]{1,0:T(8,128)S(1)} %get-tuple-element.45), channel_id=1, source_target_pairs={{0,48},{4,52},{8,56},{12,60},{16,0},{20,4},{24,8},{28,12},{32,16},... | collective-permute-start | bytes 208904 | tf_op jit(solution)/shard_map/ppermute | solution.py:592

commit v3 on v2

--- a/solution.py
+++ b/solution.py
@@ -204,12 +204,12 @@
         lo, hi = 128 * k, 128 * (k + 1)
         inverses = invert_cholesky([work[b, lo:hi, lo:hi] for b in range(count)])
         for b in range(count):
-            solved = dot_high(inverses[b], aug[b, lo:hi, :])
+            solved = dot3(inverses[b], aug[b, lo:hi, :])
             aug[b, lo:hi, :] = solved
             if hi < red:
                 panel = dot_high(work[b, hi:, lo:hi], inverses[b], NT)
                 work[b, hi:, hi:] = work[b, hi:, hi:] - dot_high(panel, panel, NT)
-                aug[b, hi:, :] = aug[b, hi:, :] - dot_high(panel, solved)
+                aug[b, hi:, :] = aug[b, hi:, :] - dot3(panel, solved)
     for b in range(count):
         solved_t = aug[b, :, dof:].T
         own_ref[b] = own_ref[b] - dot_high(solved_t, aug[b, :, dof:])
@@ -245,7 +245,10 @@
         cost_estimate=pl.CostEstimate(flops=8 << 30, bytes_accessed=6 << 20, transcendentals=0),
         interpret=interpret,
         name="factor",
-    )(self_blocks, orders, interpolation)
+    )(*[
+        pltpu.with_memory_space_constraint(x, pltpu.HBM)
+        for x in (self_blocks, orders, interpolation)
+    ])
 
 
 def pack_symmetric(block, flag):

time: 90.4 us -> 88.1 us (0.975)
  starting transfers between devices: 27.2 us -> 29 us
  local copies, waits for them, and re-layouts: 1.69 us -> 0.01 us
  Pallas kernels: 45.9 us -> 44.3 us
    unnamed x10 -> x6, local copies, waits for them, and re-layouts: 1.69 us -> 0.01 us
    pallas_call x1, Pallas kernels: 25.9 us -> 24.2 us  [factor(): pl.pallas_call(factor_kernel, out_shape=(jax.ShapeDtypeStruct((count, dof...]
    ppermute x12, starting transfers between devices: 21.5 us -> 23 us  [shifted(): return lax.ppermute(block, 'box', moves)]
  transfers between devices with their start and end apart: 15 -> 15, of which waited for: 3 -> 2; matrix products, arithmetic and copies ran while one was open for 0% -> 0% of each run, Pallas kernels for 9% -> 9%
where the time goes in v3:
time: 88.1 us
  Pallas kernels  44.3 us (50%)
  starting transfers between devices  29 us (33%)
  waiting for transfers between devices  13.9 us (16%)
    pallas_call x1, Pallas kernels, factor(): pl.pallas_call(factor_kernel, out_shape=(jax.ShapeDtypeStruct((count, dof...  24.2 us
    ppermute x12, starting transfers between devices, shifted(): return lax.ppermute(block, 'box', moves)  23 us
    ppermute x12, waiting for transfers between devices, shifted(): return lax.ppermute(block, 'box', moves)  13.9 us
    pallas_call x1, Pallas kernels, far_updates(): pl.pallas_call(functools.partial(far_kernel, caps=caps, starts=starts, bo...  8.2 us
    ppermute x3, starting transfers between devices, on_device(): sib_got.append(lax.ppermute(kept[s], 'sib', moves))  6 us
    pallas_call x1, Pallas kernels, near_updates(): pl.pallas_call(near_kernel, out_shape=[jax.ShapeDtypeStruct((count, NSIB,...  5.39 us
    pallas_call x1, Pallas kernels, couple(): pl.pallas_call(couple_kernel, out_shape=jax.ShapeDtypeStruct((count, skel...  2.91 us
    pallas_call x1, Pallas kernels, assemble(): pl.pallas_call(assemble_kernel, out_shape=jax.ShapeDtypeStruct((256, 1024...  2.01 us
  transfers between devices with their start and end apart: 15, of which 2 were waited for; matrix products, arithmetic and copies ran while one was open for 0% of the time, Pallas kernels for 9%

profile of v3, /device:TPU:8, one launch (start us, length us, event | category | flops | bytes accessed | tf_op | source)
XLA Modules:
  0.0 88.1 jit_solution(9705798203391946048)
XLA Ops:
  0.6 0.1 pad_add_fusion.where_ref
  0.7 24.2 %factor.1 = (bf16[2,512,512]{2,1,0:T(8,128)(2,1)S(1)}, bf16[2,512,512]{2,1,0:T(8,128)(2,1)S(1)}, f32[2,128,128]{2,1,0:T(8,128)S(1)}) custom-call(f32[2,512,512]{2,1,0:T(8,128)} %bitcast.15, s32[2,512]{1,0:T(2,128)} %bitcast.17, f32[2,128,384]{2,1,0:T(8,128)} %bitcast.16), custom_call_target="tpu_custom_call" | custom-call | flops 8589934592 | bytes 6291456 | tf_op jit(solution)/shard_map/factor/pallas_call | solution.py:228
  25.0 8.2 %far_updates.1 = (f32[264,128]{1,0:T(8,128)S(1)}, f32[200,128]{1,0:T(8,128)S(1)}, f32[264,128]{1,0:T(8,128)S(1)}, f32[136,128]{1,0:T(8,128)S(1)}, f32[264,128]{1...) custom-call(s32[2,16]{1,0:T(2,128)S(1)} %bitcast.12, ...), custom_call_target="tpu_custom_call" | custom-call | flops 6442450944 | bytes 8388608 | tf_op jit(solution)/shard_map/far_updates/pallas_call | solution.py:368
  33.2 0.1 collective-permute-start
  33.3 1.7 %collective-permute-start.2 = (f32[136,128]{1,0:T(8,128)S(1)}, f32[136,128]{1,0:T(8,128)S(1)}, u32[]{:S(2)}, u32[]{:S(2)}) collective-permute-start(f32[136,128]{1,0:T(8,128)S(1)} %get-tuple-element.33), channel_id=1, source_target_pairs={{0,68},{4,64},{8,76},{12,72},{16,84},{20,80},{24,92},{28,88},{32,1... | collective-permute-start | bytes 208904 | tf_op jit(solution)/shard_map/ppermute | solution.py:595
  35.0 1.3 %collective-permute-start.1 = (f32[264,128]{1,0:T(8,128)S(1)}, f32[264,128]{1,0:T(8,128)S(1)}, u32[]{:S(2)}, u32[]{:S(2)}) collective-permute-start(f32[264,128]{1,0:T(8,128)S(1)} %get-tuple-element.32), channel_id=1, source_target_pairs={{0,64},{4,68},{8,72},{12,76},{16,80},{20,84},{24,88},{28,92},{32,9... | collective-permute-start | bytes 405512 | tf_op jit(solution)/shard_map/ppermute | solution.py:595
  36.2 1.4 %collective-permute-start.3 = (f32[264,128]{1,0:T(8,128)S(1)}, f32[264,128]{1,0:T(8,128)S(1)}, u32[]{:S(2)}, u32[]{:S(2)}) collective-permute-start(f32[264,128]{1,0:T(8,128)S(1)} %get-tuple-element.34), channel_id=1, source_target_pairs={{0,128},{4,132},{8,136},{12,140},{16,144},{20,148},{24,152},{28,15... | collective-permute-start | bytes 405512 | tf_op jit(solution)/shard_map/ppermute | solution.py:595
  37.7 1.2 %collective-permute-start.4 = (f32[264,128]{1,0:T(8,128)S(1)}, f32[264,128]{1,0:T(8,128)S(1)}, u32[]{:S(2)}, u32[]{:S(2)}) collective-permute-start(f32[264,128]{1,0:T(8,128)S(1)} %get-tuple-element.35), channel_id=1, source_target_pairs={{0,132},{4,128},{8,140},{12,136},{16,148},{20,144},{24,156},{28,15... | collective-permute-start | bytes 405512 | tf_op jit(solution)/shard_map/ppermute | solution.py:595
  38.9 0.0 collective-permute-done.2.rest_3_
  38.9 1.7 %collective-permute-start.5 = (f32[264,128]{1,0:T(8,128)S(1)}, f32[264,128]{1,0:T(8,128)S(1)}, u32[]{:S(2)}, u32[]{:S(2)}) collective-permute-start(f32[264,128]{1,0:T(8,128)S(1)} %get-tuple-element.36), channel_id=1, source_target_pairs={{0,192},{4,196},{8,200},{12,204},{16,208},{20,212},{24,216},{28,22... | collective-permute-start | bytes 405512 | tf_op jit(solution)/shard_map/ppermute | solution.py:595
  40.6 1.2 %collective-permute-start.6 = (f32[200,128]{1,0:T(8,128)S(1)}, f32[200,128]{1,0:T(8,128)S(1)}, u32[]{:S(2)}, u32[]{:S(2)}) collective-permute-start(f32[200,128]{1,0:T(8,128)S(1)} %get-tuple-element.37), channel_id=1, source_target_pairs={{0,196},{4,192},{8,204},{12,200},{16,212},{20,208},{24,220},{28,21... | collective-permute-start | bytes 307208 | tf_op jit(solution)/shard_map/ppermute | solution.py:595
  41.8 9.2 %collective-permute-done.6.rest_7_ = f32[200,128]{1,0:T(8,128)S(1)} collective-permute-done((f32[200,128]{1,0:T(8,128)S(1)}, f32[200,128]{1,0:T(8,128)S(1)}, u32[]{:S(2)}, u32[]{:S(2)}) %collective-permute-start.6) | collective-permute-done | bytes 102432 | tf_op jit(solution)/shard_map/ppermute | solution.py:595
  51.0 0.0 collective-permute-done.1.rest_2_
  51.1 1.5 %route.1 = (f32[136,128]{1,0:T(8,128)S(1)}, f32[272,128]{1,0:T(8,128)S(1)}, f32[272,128]{1,0:T(8,128)S(1)}, f32[136,128]{1,0:T(8,128)S(1)}, f32[136,128]{1,0:T(8,128)S(1)}, /*index=5*/f32[136,128]{1,0:T(8,128)S(1)}) custom-call(s32[2]{0:T(128)S(1)} %pad_add_fusion.where_ref, s32[64,128]{1,0:T(8,128)S(1)} %copy-done, ...), custom_call_target="tpu_custom_call" | custom-call | flops 4194304 | bytes 2097152 | tf_op jit(solution)/shard_map/route/pallas_call | solution.py:496
  52.6 2.0 %collective-permute-start.7 = (f32[272,128]{1,0:T(8,128)S(1)}, f32[272,128]{1,0:T(8,128)S(1)}, u32[]{:S(2)}, u32[]{:S(2)}) collective-permute-start(f32[272,128]{1,0:T(8,128)S(1)} %get-tuple-element.39), channel_id=1, source_target_pairs={{0,8},{4,12},{8,16},{12,20},{16,24},{20,28},{24,32},{28,36},{32,40... | collective-permute-start | bytes 417800 | tf_op jit(solution)/shard_map/ppermute | solution.py:595
  54.6 4.0 %collective-permute-start.8 = (f32[272,128]{1,0:T(8,128)S(1)}, f32[272,128]{1,0:T(8,128)S(1)}, u32[]{:S(2)}, u32[]{:S(2)}) collective-permute-start(f32[272,128]{1,0:T(8,128)S(1)} %get-tuple-element.40), channel_id=1, source_target_pairs={{0,56},{4,60},{8,0},{12,4},{16,8},{20,12},{24,16},{28,20},{32,24},... | collective-permute-start | bytes 417800 | tf_op jit(solution)/shard_map/ppermute | solution.py:595
  58.6 5.4 %near_updates.1 = (f32[2,4,128,128]{3,2,1,0:T(8,128)S(1)}, f32[2,328,128]{2,1,0:T(8,128)S(1)}, f32[2,328,128]{2,1,0:T(8,128)S(1)}, f32[2,328,128]{2,1,0:T(8,128)S(1)}, f32[2,328,128]{2,1,0:T(8,128)S(1)}) custom-call(s32[2,16]{1,0:T(2,128)S(1)} %bitcast.13, s32[2]{0:T(128)S(1)} %pad_add_fusion.where_ref, bf16[2,512,512]{2,1,0:T(8,128)(2,1)S(1)} %get-tuple-element.26.high_ref, ...), custom_call_target="tpu_custom_call" | custom-call | flops 3221225472 | bytes 8388608 | tf_op jit(solution)/shard_map/near_updates/pallas_call | solution.py:423
  64.0 1.8 %collective-permute-start.12 = (f32[2,328,128]{2,1,0:T(8,128)S(1)}, f32[2,328,128]{2,1,0:T(8,128)S(1)}, u32[]{:S(2)}, u32[]{:S(2)}) collective-permute-start(f32[2,328,128]{2,1,0:T(8,128)S(1)} %get-tuple-element.47.rest_7_), channel_id=1, source_target_pairs={{0,1},{1,2},{2,3},{3,0},{4,5},{5,6},{6,7},{7,4},{8,9},{9,10},{10,1... | collective-permute-start | bytes 1007624 | tf_op jit(solution)/shard_map/ppermute | solution.py:604
  65.8 2.7 %collective-permute-start.13 = (f32[2,328,128]{2,1,0:T(8,128)S(1)}, f32[2,328,128]{2,1,0:T(8,128)S(1)}, u32[]{:S(2)}, u32[]{:S(2)}) collective-permute-start(f32[2,328,128]{2,1,0:T(8,128)S(1)} %get-tuple-element.48.rest_8_), channel_id=1, source_target_pairs={{0,2},{1,3},{2,0},{3,1},{4,6},{5,7},{6,4},{7,5},{8,10},{9,11},{10,... | collective-permute-start | bytes 1007624 | tf_op jit(solution)/shard_map/ppermute | solution.py:604
  68.6 1.4 %collective-permute-start.14 = (f32[2,328,128]{2,1,0:T(8,128)S(1)}, f32[2,328,128]{2,1,0:T(8,128)S(1)}, u32[]{:S(2)}, u32[]{:S(2)}) collective-permute-start(f32[2,328,128]{2,1,0:T(8,128)S(1)} %get-tuple-element.49.rest_9_), channel_id=1, source_target_pairs={{0,3},{1,0},{2,1},{3,2},{4,7},{5,4},{6,5},{7,6},{8,11},{9,8},{10,9... | collective-permute-start | bytes 1007624 | tf_op jit(solution)/shard_map/ppermute | solution.py:604
  70.0 0.0 collective-permute-done.7.up_ref.rest_1_
  70.0 4.5 %collective-permute-start.9 = (f32[136,128]{1,0:T(8,128)S(1)}, f32[136,128]{1,0:T(8,128)S(1)}, u32[]{:S(2)}, u32[]{:S(2)}) collective-permute-start(f32[136,128]{1,0:T(8,128)S(1)} %get-tuple-element.41), channel_id=1, source_target_pairs={{0,32},{4,36},{8,40},{12,44},{16,48},{20,52},{24,56},{28,60},{32,0... | collective-permute-start | bytes 208904 | tf_op jit(solution)/shard_map/ppermute | solution.py:595
  74.5 0.0 collective-permute-done.8.down_ref.rest_2_
  74.5 0.3 collective-permute-start.10
  74.9 4.7 %collective-permute-done.9.rest_3_ = f32[136,128]{1,0:T(8,128)S(1)} collective-permute-done((f32[136,128]{1,0:T(8,128)S(1)}, f32[136,128]{1,0:T(8,128)S(1)}, u32[]{:S(2)}, u32[]{:S(2)}) %collective-permute-start.9) | collective-permute-done | bytes 69664 | tf_op jit(solution)/shard_map/ppermute | solution.py:595
  79.5 3.6 %collective-permute-start.11 = (f32[136,128]{1,0:T(8,128)S(1)}, f32[136,128]{1,0:T(8,128)S(1)}, u32[]{:S(2)}, u32[]{:S(2)}) collective-permute-start(f32[136,128]{1,0:T(8,128)S(1)} %get-tuple-element.45), channel_id=1, source_target_pairs={{0,48},{4,52},{8,56},{12,60},{16,0},{20,4},{24,8},{28,12},{32,16},... | collective-permute-start | bytes 208904 | tf_op jit(solution)/shard_map/ppermute | solution.py:595
  83.1 2.9 %couple.1 = bf16[2,128,16,128]{3,2,1,0:T(8,128)(2,1)} custom-call(bf16[2,512,512]{2,1,0:T(8,128)(2,1)S(1)} %get-tuple-element.26.high_ref, bf16[2,512,512]{2,1,0:T(8,128)(2,1)S(1)} %get-tuple-element.27.low_ref, f32[2,4,128,128]{3,2,1,0:T(8,128)S(1)} %get-tuple-element.28.near_ref, bf16[2,512,16,128]{3,2,1,0:T(8,128)(2,1)S(1)} %bitcast.11), custom_call_target="tpu_custom_call" | custom-call | flops 2147483648 | bytes 6291456 | tf_op jit(solution)/shard_map/couple/pallas_call | solution.py:455
  86.0 0.0 collective-permute-done.12.rest_10_
  86.0 0.0 collective-permute-done.13.rest_11_
  86.0 0.0 collective-permute-done.14.rest_12_
  86.0 0.0 collective-permute-done.11.rest_5_
  86.1 2.0 %assemble.1 = f32[256,1024]{1,0:T(8,128)} custom-call(s32[2]{0:T(128)S(1)} %pad_add_fusion.where_ref, f32[2,128,128]{2,1,0:T(8,128)S(1)} %get-tuple-element.29.own_ref, f32[136,128]{1,0:T(8,128)S(1)} %get-tuple-element.38.rest_0_, f32[272,128]{1,0:T(8,128)S(1)} %collective-permute-done.7.up_ref.rest_1_, ...), custom_call_target="tpu_custom_call" | custom-call | tf_op jit(solution)/shard_map/assemble/pallas_call | solution.py:566
  (12 shorter events, 0.0 us)
Async XLA Ops:
  0.7 24.2 %copy-start = (s32[64,128]{1,0:T(8,128)S(1)}, s32[64,128]{1,0:T(8,128)}, u32[]{:S(2)}) copy-start(s32[64,128]{1,0:T(8,128)} %constant.11.clone.table_ref) | copy-start | bytes 98308
  0.7 24.2 %copy-start.1 = (bf16[1,2,512,16,128]{4,3,2,1,0:T(8,128)(2,1)S(1)}, bf16[1,2,512,16,128]{4,3,2,1,0:T(8,128)(2,1)}, u32[]{:S(2)}) copy-start(bf16[1,2,512,16,128]{4,3,2,1,0:T(8,128)(2,1)} %param.9) | copy-start | bytes 12582916
  0.7 24.2 %copy-start.2 = (s32[1,2,16]{2,1,0:T(2,128)S(1)}, s32[1,2,16]{2,1,0:T(2,128)}, u32[]{:S(2)}) copy-start(s32[1,2,16]{2,1,0:T(2,128)} %param.10) | copy-start | bytes 388
  33.2 7.4 %collective-permute-start = (f32[200,128]{1,0:T(8,128)S(1)}, f32[200,128]{1,0:T(8,128)S(1)}, u32[]{:S(2)}, u32[]{:S(2)}) collective-permute-start(f32[200,128]{1,0:T(8,128)S(1)} %get-tuple-element.31), channel_id=1, source_target_pairs={{0,4},{4,0},{8,12},{12,8},{16,20},{20,16},{24,28},{28,24},{32,36},... | collective-permute-start | bytes 307208 | tf_op jit(solution)/shard_map/ppermute | solution.py:595
  33.3 5.6 %collective-permute-start.2 = (f32[136,128]{1,0:T(8,128)S(1)}, f32[136,128]{1,0:T(8,128)S(1)}, u32[]{:S(2)}, u32[]{:S(2)}) collective-permute-start(f32[136,128]{1,0:T(8,128)S(1)} %get-tuple-element.33), channel_id=1, source_target_pairs={{0,68},{4,64},{8,76},{12,72},{16,84},{20,80},{24,92},{28,88},{32,1... | collective-permute-start | bytes 208904 | tf_op jit(solution)/shard_map/ppermute | solution.py:595
  35.0 16.1 %collective-permute-start.1 = (f32[264,128]{1,0:T(8,128)S(1)}, f32[264,128]{1,0:T(8,128)S(1)}, u32[]{:S(2)}, u32[]{:S(2)}) collective-permute-start(f32[264,128]{1,0:T(8,128)S(1)} %get-tuple-element.32), channel_id=1, source_target_pairs={{0,64},{4,68},{8,72},{12,76},{16,80},{20,84},{24,88},{28,92},{32,9... | collective-permute-start | bytes 405512 | tf_op jit(solution)/shard_map/ppermute | solution.py:595
  36.2 14.8 %collective-permute-start.3 = (f32[264,128]{1,0:T(8,128)S(1)}, f32[264,128]{1,0:T(8,128)S(1)}, u32[]{:S(2)}, u32[]{:S(2)}) collective-permute-start(f32[264,128]{1,0:T(8,128)S(1)} %get-tuple-element.34), channel_id=1, source_target_pairs={{0,128},{4,132},{8,136},{12,140},{16,144},{20,148},{24,152},{28,15... | collective-permute-start | bytes 405512 | tf_op jit(solution)/shard_map/ppermute | solution.py:595
  37.7 13.4 %collective-permute-start.4 = (f32[264,128]{1,0:T(8,128)S(1)}, f32[264,128]{1,0:T(8,128)S(1)}, u32[]{:S(2)}, u32[]{:S(2)}) collective-permute-start(f32[264,128]{1,0:T(8,128)S(1)} %get-tuple-element.35), channel_id=1, source_target_pairs={{0,132},{4,128},{8,140},{12,136},{16,148},{20,144},{24,156},{28,15... | collective-permute-start | bytes 405512 | tf_op jit(solution)/shard_map/ppermute | solution.py:595
  38.9 12.1 %collective-permute-start.5 = (f32[264,128]{1,0:T(8,128)S(1)}, f32[264,128]{1,0:T(8,128)S(1)}, u32[]{:S(2)}, u32[]{:S(2)}) collective-permute-start(f32[264,128]{1,0:T(8,128)S(1)} %get-tuple-element.36), channel_id=1, source_target_pairs={{0,192},{4,196},{8,200},{12,204},{16,208},{20,212},{24,216},{28,22... | collective-permute-start | bytes 405512 | tf_op jit(solution)/shard_map/ppermute | solution.py:595
  40.6 10.4 %collective-permute-start.6 = (f32[200,128]{1,0:T(8,128)S(1)}, f32[200,128]{1,0:T(8,128)S(1)}, u32[]{:S(2)}, u32[]{:S(2)}) collective-permute-start(f32[200,128]{1,0:T(8,128)S(1)} %get-tuple-element.37), channel_id=1, source_target_pairs={{0,196},{4,192},{8,204},{12,200},{16,212},{20,208},{24,220},{28,21... | collective-permute-start | bytes 307208 | tf_op jit(solution)/shard_map/ppermute | solution.py:595
  52.6 17.4 %collective-permute-start.7 = (f32[272,128]{1,0:T(8,128)S(1)}, f32[272,128]{1,0:T(8,128)S(1)}, u32[]{:S(2)}, u32[]{:S(2)}) collective-permute-start(f32[272,128]{1,0:T(8,128)S(1)} %get-tuple-element.39), channel_id=1, source_target_pairs={{0,8},{4,12},{8,16},{12,20},{16,24},{20,28},{24,32},{28,36},{32,40... | collective-permute-start | bytes 417800 | tf_op jit(solution)/shard_map/ppermute | solution.py:595
  54.6 19.9 %collective-permute-start.8 = (f32[272,128]{1,0:T(8,128)S(1)}, f32[272,128]{1,0:T(8,128)S(1)}, u32[]{:S(2)}, u32[]{:S(2)}) collective-permute-start(f32[272,128]{1,0:T(8,128)S(1)} %get-tuple-element.40), channel_id=1, source_target_pairs={{0,56},{4,60},{8,0},{12,4},{16,8},{20,12},{24,16},{28,20},{32,24},... | collective-permute-start | bytes 417800 | tf_op jit(solution)/shard_map/ppermute | solution.py:595
  64.0 22.0 %collective-permute-start.12 = (f32[2,328,128]{2,1,0:T(8,128)S(1)}, f32[2,328,128]{2,1,0:T(8,128)S(1)}, u32[]{:S(2)}, u32[]{:S(2)}) collective-permute-start(f32[2,328,128]{2,1,0:T(8,128)S(1)} %get-tuple-element.47.rest_7_), channel_id=1, source_target_pairs={{0,1},{1,2},{2,3},{3,0},{4,5},{5,6},{6,7},{7,4},{8,9},{9,10},{10,1... | collective-permute-start | bytes 1007624 | tf_op jit(solution)/shard_map/ppermute | solution.py:604
  65.8 20.2 %collective-permute-start.13 = (f32[2,328,128]{2,1,0:T(8,128)S(1)}, f32[2,328,128]{2,1,0:T(8,128)S(1)}, u32[]{:S(2)}, u32[]{:S(2)}) collective-permute-start(f32[2,328,128]{2,1,0:T(8,128)S(1)} %get-tuple-element.48.rest_8_), channel_id=1, source_target_pairs={{0,2},{1,3},{2,0},{3,1},{4,6},{5,7},{6,4},{7,5},{8,10},{9,11},{10,... | collective-permute-start | bytes 1007624 | tf_op jit(solution)/shard_map/ppermute | solution.py:604
  68.6 17.5 %collective-permute-start.14 = (f32[2,328,128]{2,1,0:T(8,128)S(1)}, f32[2,328,128]{2,1,0:T(8,128)S(1)}, u32[]{:S(2)}, u32[]{:S(2)}) collective-permute-start(f32[2,328,128]{2,1,0:T(8,128)S(1)} %get-tuple-element.49.rest_9_), channel_id=1, source_target_pairs={{0,3},{1,0},{2,1},{3,2},{4,7},{5,4},{6,5},{7,6},{8,11},{9,8},{10,9... | collective-permute-start | bytes 1007624 | tf_op jit(solution)/shard_map/ppermute | solution.py:604
  70.0 9.5 %collective-permute-start.9 = (f32[136,128]{1,0:T(8,128)S(1)}, f32[136,128]{1,0:T(8,128)S(1)}, u32[]{:S(2)}, u32[]{:S(2)}) collective-permute-start(f32[136,128]{1,0:T(8,128)S(1)} %get-tuple-element.41), channel_id=1, source_target_pairs={{0,32},{4,36},{8,40},{12,44},{16,48},{20,52},{24,56},{28,60},{32,0... | collective-permute-start | bytes 208904 | tf_op jit(solution)/shard_map/ppermute | solution.py:595
  74.5 11.5 %collective-permute-start.10 = (f32[136,128]{1,0:T(8,128)S(1)}, f32[136,128]{1,0:T(8,128)S(1)}, u32[]{:S(2)}, u32[]{:S(2)}) collective-permute-start(f32[136,128]{1,0:T(8,128)S(1)} %get-tuple-element.44), channel_id=1, source_target_pairs={{0,16},{4,20},{8,24},{12,28},{16,32},{20,36},{24,40},{28,44},{32,4... | collective-permute-start | bytes 208904 | tf_op jit(solution)/shard_map/ppermute | solution.py:595
  79.5 6.5 %collective-permute-start.11 = (f32[136,128]{1,0:T(8,128)S(1)}, f32[136,128]{1,0:T(8,128)S(1)}, u32[]{:S(2)}, u32[]{:S(2)}) collective-permute-start(f32[136,128]{1,0:T(8,128)S(1)} %get-tuple-element.45), channel_id=1, source_target_pairs={{0,48},{4,52},{8,56},{12,60},{16,0},{20,4},{24,8},{28,12},{32,16},... | collective-permute-start | bytes 208904 | tf_op jit(solution)/shard_map/ppermute | solution.py:595

commit v4 on v3

--- a/solution.py
+++ b/solution.py
@@ -322,57 +322,48 @@
     return dot_bf16(high, high, NT) + (dot_bf16(high, low, NT) + dot_bf16(low, high, NT))
 
 
-def slot_updates(high_ref, low_ref, slot_pair):
-    product = dot_bf16(high_ref[0], slot_pair) + dot_bf16(low_ref[0], slot_pair)
-    both = gram(product.T)
+def slot_updates(high, low, slot_pair):
+    both = gram((dot_bf16(high, slot_pair) + dot_bf16(low, slot_pair)).T)
     return both[:128, :128], both[128:, 128:]
 
 
 def far_kernel(ids_ref, where_ref, table_ref, high_ref, low_ref, w_ref, *rest, caps, starts, boxes):
     outs, (bodies, tails) = rest[: len(caps)], rest[len(caps) :]
-    box = pl.program_id(0)
     parent = where_ref[0]
-
-    @pl.when(box == 0)
-    def _():
-        bodies[...] = jnp.zeros_like(bodies)
-        tails[...] = jnp.zeros_like(tails)
-
-    slots = w_ref.shape[2]
-    by_slot = jnp.swapaxes(w_ref[0], 0, 1)
-    for first in range(NSIB, slots, 2):
-        pair = jnp.concatenate([by_slot[first], by_slot[first + 1]], axis=1)
-        for s, update in enumerate(slot_updates(high_ref, low_ref, pair)):
-            other = ids_ref[box, first + s]
-            body, tail = pack_symmetric(update, (other & 1).astype(F32))
-            place = table_ref[parent & 7, ((other >> 3) - parent) & (boxes - 1)]
-            bodies[place] = body
-            tails[pl.ds(place, 1), :] = tail
-
-    @pl.when(box == pl.num_programs(0) - 1)
-    def _():
-        for s, out in enumerate(outs):
-            for j in range(caps[s]):
-                out[64 * j : 64 * j + 64] = bodies[starts[s] + j]
-            out[64 * caps[s] : 64 * caps[s] + 8] = jnp.concatenate(
-                [tails[starts[s] : starts[s] + caps[s]], jnp.zeros((8 - caps[s], 128), F32)], axis=0
-            )
+    bodies[...] = jnp.zeros_like(bodies)
+    tails[...] = jnp.zeros_like(tails)
+    count, _, slots, _ = w_ref.shape
+    for box in range(count):
+        by_slot = jnp.swapaxes(w_ref[box], 0, 1)
+        for first in range(NSIB, slots, 2):
+            pair = jnp.concatenate([by_slot[first], by_slot[first + 1]], axis=1)
+            for s, update in enumerate(slot_updates(high_ref[box], low_ref[box], pair)):
+                other = ids_ref[box, first + s]
+                body, tail = pack_symmetric(update, (other & 1).astype(F32))
+                place = table_ref[parent & 7, ((other >> 3) - parent) & (boxes - 1)]
+                bodies[place] = body
+                tails[pl.ds(place, 1), :] = tail
+    for s, out in enumerate(outs):
+        for j in range(caps[s]):
+            out[64 * j : 64 * j + 64] = bodies[starts[s] + j]
+        out[64 * caps[s] : 64 * caps[s] + 8] = jnp.concatenate(
+            [tails[starts[s] : starts[s] + caps[s]], jnp.zeros((8 - caps[s], 128), F32)], axis=0
+        )
 
 
 def far_updates(ids, where, table, high, low, w, caps, starts, boxes, interpret=False):
-    count, dof, slots, skel = w.shape
+    count, dof, _, skel = w.shape
     red = dof - skel
     whole = lambda shape: pl.BlockSpec(shape, lambda b, *_: (0,) * len(shape))
-    by_box = lambda shape: pl.BlockSpec((1,) + shape, lambda b, *_: (b,) + (0,) * len(shape))
     outs = [(64 * cap + 8, 128) for cap in caps]
     return pl.pallas_call(
         functools.partial(far_kernel, caps=caps, starts=starts, boxes=boxes),
         out_shape=[jax.ShapeDtypeStruct(shape, F32) for shape in outs],
         grid_spec=pltpu.PrefetchScalarGridSpec(
             num_scalar_prefetch=2,
-            grid=(count,),
+            grid=(1,),
             in_specs=[row_spec(table)]
-            + [by_box((red, dof)), by_box((red, dof)), by_box((dof, slots, skel))],
+            + [whole((count, red, dof)), whole((count, red, dof)), whole(w.shape)],
             out_specs=[whole(shape) for shape in outs],
             scratch_shapes=[
                 pltpu.VMEM((starts[-1], 64, 128), F32),

time: 88.1 us -> 86.3 us (0.980)
  starting transfers between devices: 29 us -> 27.2 us
  Pallas kernels: 44.3 us -> 43.4 us
    ppermute x12, starting transfers between devices: 23 us -> 21.5 us  [shifted(): return lax.ppermute(block, 'box', moves)]
  transfers between devices with their start and end apart: 15 -> 15, of which waited for: 2 -> 3; matrix products, arithmetic and copies ran while one was open for 0% -> 0% of each run, Pallas kernels for 9% -> 10%
where the time goes in v4:
time: 86.3 us; the launch traced here: 86.2 us
  Pallas kernels  43.4 us (50%)
  starting transfers between devices  27.2 us (32%)
  waiting for transfers between devices  14.7 us (17%)
    pallas_call x1, Pallas kernels, factor(): pl.pallas_call(factor_kernel, out_shape=(jax.ShapeDtypeStruct((count, dof...  24.2 us
    ppermute x12, starting transfers between devices, shifted(): return lax.ppermute(block, 'box', moves)  21.5 us
    ppermute x12, waiting for transfers between devices, shifted(): return lax.ppermute(block, 'box', moves)  14.7 us
    pallas_call x1, Pallas kernels, far_updates(): pl.pallas_call(functools.partial(far_kernel, caps=caps, starts=starts, bo...  7.36 us
    ppermute x3, starting transfers between devices, on_device(): sib_got.append(lax.ppermute(kept[s], 'sib', moves))  5.74 us
    pallas_call x1, Pallas kernels, near_updates(): pl.pallas_call(near_kernel, out_shape=[jax.ShapeDtypeStruct((count, NSIB,...  5.39 us
    pallas_call x1, Pallas kernels, couple(): pl.pallas_call(couple_kernel, out_shape=jax.ShapeDtypeStruct((count, skel...  2.91 us
    pallas_call x1, Pallas kernels, assemble(): pl.pallas_call(assemble_kernel, out_shape=jax.ShapeDtypeStruct((256, 1024...  2 us
  transfers between devices with their start and end apart: 15, of which 3 were waited for; matrix products, arithmetic and copies ran while one was open for 0% of the time, Pallas kernels for 10%

profile of v4, /device:TPU:8, one launch (start us, length us, event | category | flops | bytes accessed | tf_op | source)
XLA Modules:
  0.0 86.2 jit_solution(3974010806307978148)
XLA Ops:
  0.6 0.1 pad_add_fusion.where_ref
  0.7 24.2 %factor.1 = (bf16[2,512,512]{2,1,0:T(8,128)(2,1)S(1)}, bf16[2,512,512]{2,1,0:T(8,128)(2,1)S(1)}, f32[2,128,128]{2,1,0:T(8,128)S(1)}) custom-call(f32[2,512,512]{2,1,0:T(8,128)} %bitcast.15, s32[2,512]{1,0:T(2,128)} %bitcast.17, f32[2,128,384]{2,1,0:T(8,128)} %bitcast.16), custom_call_target="tpu_custom_call" | custom-call | flops 8589934592 | bytes 6291456 | tf_op jit(solution)/shard_map/factor/pallas_call | solution.py:228
  25.0 7.4 %far_updates.1 = (f32[264,128]{1,0:T(8,128)S(1)}, f32[200,128]{1,0:T(8,128)S(1)}, f32[264,128]{1,0:T(8,128)S(1)}, f32[136,128]{1,0:T(8,128)S(1)}, f32[264,128]{1...) custom-call(s32[2,16]{1,0:T(2,128)S(1)} %bitcast.12, ...), custom_call_target="tpu_custom_call" | custom-call | flops 6442450944 | bytes 8388608 | tf_op jit(solution)/shard_map/far_updates/pallas_call | solution.py:359
  32.3 0.1 collective-permute-start
  32.4 1.7 %collective-permute-start.2 = (f32[136,128]{1,0:T(8,128)S(1)}, f32[136,128]{1,0:T(8,128)S(1)}, u32[]{:S(2)}, u32[]{:S(2)}) collective-permute-start(f32[136,128]{1,0:T(8,128)S(1)} %get-tuple-element.33), channel_id=1, source_target_pairs={{0,68},{4,64},{8,76},{12,72},{16,84},{20,80},{24,92},{28,88},{32,1... | collective-permute-start | bytes 208904 | tf_op jit(solution)/shard_map/ppermute | solution.py:586
  34.1 1.3 %collective-permute-start.1 = (f32[264,128]{1,0:T(8,128)S(1)}, f32[264,128]{1,0:T(8,128)S(1)}, u32[]{:S(2)}, u32[]{:S(2)}) collective-permute-start(f32[264,128]{1,0:T(8,128)S(1)} %get-tuple-element.32), channel_id=1, source_target_pairs={{0,64},{4,68},{8,72},{12,76},{16,80},{20,84},{24,88},{28,92},{32,9... | collective-permute-start | bytes 405512 | tf_op jit(solution)/shard_map/ppermute | solution.py:586
  35.4 1.4 %collective-permute-start.3 = (f32[264,128]{1,0:T(8,128)S(1)}, f32[264,128]{1,0:T(8,128)S(1)}, u32[]{:S(2)}, u32[]{:S(2)}) collective-permute-start(f32[264,128]{1,0:T(8,128)S(1)} %get-tuple-element.34), channel_id=1, source_target_pairs={{0,128},{4,132},{8,136},{12,140},{16,144},{20,148},{24,152},{28,15... | collective-permute-start | bytes 405512 | tf_op jit(solution)/shard_map/ppermute | solution.py:586
  36.8 1.2 %collective-permute-start.4 = (f32[264,128]{1,0:T(8,128)S(1)}, f32[264,128]{1,0:T(8,128)S(1)}, u32[]{:S(2)}, u32[]{:S(2)}) collective-permute-start(f32[264,128]{1,0:T(8,128)S(1)} %get-tuple-element.35), channel_id=1, source_target_pairs={{0,132},{4,128},{8,140},{12,136},{16,148},{20,144},{24,156},{28,15... | collective-permute-start | bytes 405512 | tf_op jit(solution)/shard_map/ppermute | solution.py:586
  38.1 0.0 collective-permute-done.2.rest_3_
  38.1 1.7 %collective-permute-start.5 = (f32[264,128]{1,0:T(8,128)S(1)}, f32[264,128]{1,0:T(8,128)S(1)}, u32[]{:S(2)}, u32[]{:S(2)}) collective-permute-start(f32[264,128]{1,0:T(8,128)S(1)} %get-tuple-element.36), channel_id=1, source_target_pairs={{0,192},{4,196},{8,200},{12,204},{16,208},{20,212},{24,216},{28,22... | collective-permute-start | bytes 405512 | tf_op jit(solution)/shard_map/ppermute | solution.py:586
  39.8 1.2 %collective-permute-start.6 = (f32[200,128]{1,0:T(8,128)S(1)}, f32[200,128]{1,0:T(8,128)S(1)}, u32[]{:S(2)}, u32[]{:S(2)}) collective-permute-start(f32[200,128]{1,0:T(8,128)S(1)} %get-tuple-element.37), channel_id=1, source_target_pairs={{0,196},{4,192},{8,204},{12,200},{16,212},{20,208},{24,220},{28,21... | collective-permute-start | bytes 307208 | tf_op jit(solution)/shard_map/ppermute | solution.py:586
  41.0 9.2 %collective-permute-done.6.rest_7_ = f32[200,128]{1,0:T(8,128)S(1)} collective-permute-done((f32[200,128]{1,0:T(8,128)S(1)}, f32[200,128]{1,0:T(8,128)S(1)}, u32[]{:S(2)}, u32[]{:S(2)}) %collective-permute-start.6) | collective-permute-done | bytes 102432 | tf_op jit(solution)/shard_map/ppermute | solution.py:586
  50.2 0.0 collective-permute-done.1.rest_2_
  50.2 0.0 collective-permute-done.3.rest_4_
  50.2 1.5 %route.1 = (f32[136,128]{1,0:T(8,128)S(1)}, f32[272,128]{1,0:T(8,128)S(1)}, f32[272,128]{1,0:T(8,128)S(1)}, f32[136,128]{1,0:T(8,128)S(1)}, f32[136,128]{1,0:T(8,128)S(1)}, /*index=5*/f32[136,128]{1,0:T(8,128)S(1)}) custom-call(s32[2]{0:T(128)S(1)} %pad_add_fusion.where_ref, s32[64,128]{1,0:T(8,128)S(1)} %copy-done, ...), custom_call_target="tpu_custom_call" | custom-call | flops 4194304 | bytes 2097152 | tf_op jit(solution)/shard_map/route/pallas_call | solution.py:487
  51.8 2.0 %collective-permute-start.7 = (f32[272,128]{1,0:T(8,128)S(1)}, f32[272,128]{1,0:T(8,128)S(1)}, u32[]{:S(2)}, u32[]{:S(2)}) collective-permute-start(f32[272,128]{1,0:T(8,128)S(1)} %get-tuple-element.39), channel_id=1, source_target_pairs={{0,8},{4,12},{8,16},{12,20},{16,24},{20,28},{24,32},{28,36},{32,40... | collective-permute-start | bytes 417800 | tf_op jit(solution)/shard_map/ppermute | solution.py:586
  53.8 4.3 %collective-permute-start.8 = (f32[272,128]{1,0:T(8,128)S(1)}, f32[272,128]{1,0:T(8,128)S(1)}, u32[]{:S(2)}, u32[]{:S(2)}) collective-permute-start(f32[272,128]{1,0:T(8,128)S(1)} %get-tuple-element.40), channel_id=1, source_target_pairs={{0,56},{4,60},{8,0},{12,4},{16,8},{20,12},{24,16},{28,20},{32,24},... | collective-permute-start | bytes 417800 | tf_op jit(solution)/shard_map/ppermute | solution.py:586
  58.0 5.4 %near_updates.1 = (f32[2,4,128,128]{3,2,1,0:T(8,128)S(1)}, f32[2,328,128]{2,1,0:T(8,128)S(1)}, f32[2,328,128]{2,1,0:T(8,128)S(1)}, f32[2,328,128]{2,1,0:T(8,128)S(1)}, f32[2,328,128]{2,1,0:T(8,128)S(1)}) custom-call(s32[2,16]{1,0:T(2,128)S(1)} %bitcast.13, s32[2]{0:T(128)S(1)} %pad_add_fusion.where_ref, bf16[2,512,512]{2,1,0:T(8,128)(2,1)S(1)} %get-tuple-element.26.high_ref, ...), custom_call_target="tpu_custom_call" | custom-call | flops 3221225472 | bytes 8388608 | tf_op jit(solution)/shard_map/near_updates/pallas_call | solution.py:414
  63.4 1.6 %collective-permute-start.12 = (f32[2,328,128]{2,1,0:T(8,128)S(1)}, f32[2,328,128]{2,1,0:T(8,128)S(1)}, u32[]{:S(2)}, u32[]{:S(2)}) collective-permute-start(f32[2,328,128]{2,1,0:T(8,128)S(1)} %get-tuple-element.47.rest_7_), channel_id=1, source_target_pairs={{0,1},{1,2},{2,3},{3,0},{4,5},{5,6},{6,7},{7,4},{8,9},{9,10},{10,1... | collective-permute-start | bytes 1007624 | tf_op jit(solution)/shard_map/ppermute | solution.py:595
  65.0 2.7 %collective-permute-start.13 = (f32[2,328,128]{2,1,0:T(8,128)S(1)}, f32[2,328,128]{2,1,0:T(8,128)S(1)}, u32[]{:S(2)}, u32[]{:S(2)}) collective-permute-start(f32[2,328,128]{2,1,0:T(8,128)S(1)} %get-tuple-element.48.rest_8_), channel_id=1, source_target_pairs={{0,2},{1,3},{2,0},{3,1},{4,6},{5,7},{6,4},{7,5},{8,10},{9,11},{10,... | collective-permute-start | bytes 1007624 | tf_op jit(solution)/shard_map/ppermute | solution.py:595
  67.7 1.4 %collective-permute-start.14 = (f32[2,328,128]{2,1,0:T(8,128)S(1)}, f32[2,328,128]{2,1,0:T(8,128)S(1)}, u32[]{:S(2)}, u32[]{:S(2)}) collective-permute-start(f32[2,328,128]{2,1,0:T(8,128)S(1)} %get-tuple-element.49.rest_9_), channel_id=1, source_target_pairs={{0,3},{1,0},{2,1},{3,2},{4,7},{5,4},{6,5},{7,6},{8,11},{9,8},{10,9... | collective-permute-start | bytes 1007624 | tf_op jit(solution)/shard_map/ppermute | solution.py:595
  69.2 0.0 collective-permute-done.7.up_ref.rest_1_
  69.2 4.2 %collective-permute-start.9 = (f32[136,128]{1,0:T(8,128)S(1)}, f32[136,128]{1,0:T(8,128)S(1)}, u32[]{:S(2)}, u32[]{:S(2)}) collective-permute-start(f32[136,128]{1,0:T(8,128)S(1)} %get-tuple-element.41), channel_id=1, source_target_pairs={{0,32},{4,36},{8,40},{12,44},{16,48},{20,52},{24,56},{28,60},{32,0... | collective-permute-start | bytes 208904 | tf_op jit(solution)/shard_map/ppermute | solution.py:586
  73.4 0.3 collective-permute-start.10
  73.8 5.2 %collective-permute-done.9.rest_3_ = f32[136,128]{1,0:T(8,128)S(1)} collective-permute-done((f32[136,128]{1,0:T(8,128)S(1)}, f32[136,128]{1,0:T(8,128)S(1)}, u32[]{:S(2)}, u32[]{:S(2)}) %collective-permute-start.9) | collective-permute-done | bytes 69664 | tf_op jit(solution)/shard_map/ppermute | solution.py:586
  79.0 2.0 %collective-permute-start.11 = (f32[136,128]{1,0:T(8,128)S(1)}, f32[136,128]{1,0:T(8,128)S(1)}, u32[]{:S(2)}, u32[]{:S(2)}) collective-permute-start(f32[136,128]{1,0:T(8,128)S(1)} %get-tuple-element.45), channel_id=1, source_target_pairs={{0,48},{4,52},{8,56},{12,60},{16,0},{20,4},{24,8},{28,12},{32,16},... | collective-permute-start | bytes 208904 | tf_op jit(solution)/shard_map/ppermute | solution.py:586
  81.0 2.9 %couple.1 = bf16[2,128,16,128]{3,2,1,0:T(8,128)(2,1)} custom-call(bf16[2,512,512]{2,1,0:T(8,128)(2,1)S(1)} %get-tuple-element.26.high_ref, bf16[2,512,512]{2,1,0:T(8,128)(2,1)S(1)} %get-tuple-element.27.low_ref, f32[2,4,128,128]{3,2,1,0:T(8,128)S(1)} %get-tuple-element.28.near_ref, bf16[2,512,16,128]{3,2,1,0:T(8,128)(2,1)S(1)} %bitcast.11), custom_call_target="tpu_custom_call" | custom-call | flops 2147483648 | bytes 6291456 | tf_op jit(solution)/shard_map/couple/pallas_call | solution.py:446
  83.9 0.0 collective-permute-done.12.rest_10_
  83.9 0.0 collective-permute-done.13.rest_11_
  83.9 0.0 collective-permute-done.14.rest_12_
  83.9 0.2 collective-permute-done.11.rest_5_
  84.2 2.0 %assemble.1 = f32[256,1024]{1,0:T(8,128)} custom-call(s32[2]{0:T(128)S(1)} %pad_add_fusion.where_ref, f32[2,128,128]{2,1,0:T(8,128)S(1)} %get-tuple-element.29.own_ref, f32[136,128]{1,0:T(8,128)S(1)} %get-tuple-element.38.rest_0_, f32[272,128]{1,0:T(8,128)S(1)} %collective-permute-done.7.up_ref.rest_1_, ...), custom_call_target="tpu_custom_call" | custom-call | tf_op jit(solution)/shard_map/assemble/pallas_call | solution.py:557
  (12 shorter events, 0.0 us)
Async XLA Ops:
  0.7 24.2 %copy-start = (s32[64,128]{1,0:T(8,128)S(1)}, s32[64,128]{1,0:T(8,128)}, u32[]{:S(2)}) copy-start(s32[64,128]{1,0:T(8,128)} %constant.11.clone.table_ref) | copy-start | bytes 98308
  0.7 24.2 %copy-start.1 = (bf16[1,2,512,16,128]{4,3,2,1,0:T(8,128)(2,1)S(1)}, bf16[1,2,512,16,128]{4,3,2,1,0:T(8,128)(2,1)}, u32[]{:S(2)}) copy-start(bf16[1,2,512,16,128]{4,3,2,1,0:T(8,128)(2,1)} %param.9) | copy-start | bytes 12582916
  0.7 24.2 %copy-start.2 = (s32[1,2,16]{2,1,0:T(2,128)S(1)}, s32[1,2,16]{2,1,0:T(2,128)}, u32[]{:S(2)}) copy-start(s32[1,2,16]{2,1,0:T(2,128)} %param.10) | copy-start | bytes 388
  32.3 7.4 %collective-permute-start = (f32[200,128]{1,0:T(8,128)S(1)}, f32[200,128]{1,0:T(8,128)S(1)}, u32[]{:S(2)}, u32[]{:S(2)}) collective-permute-start(f32[200,128]{1,0:T(8,128)S(1)} %get-tuple-element.31), channel_id=1, source_target_pairs={{0,4},{4,0},{8,12},{12,8},{16,20},{20,16},{24,28},{28,24},{32,36},... | collective-permute-start | bytes 307208 | tf_op jit(solution)/shard_map/ppermute | solution.py:586
  32.4 5.6 %collective-permute-start.2 = (f32[136,128]{1,0:T(8,128)S(1)}, f32[136,128]{1,0:T(8,128)S(1)}, u32[]{:S(2)}, u32[]{:S(2)}) collective-permute-start(f32[136,128]{1,0:T(8,128)S(1)} %get-tuple-element.33), channel_id=1, source_target_pairs={{0,68},{4,64},{8,76},{12,72},{16,84},{20,80},{24,92},{28,88},{32,1... | collective-permute-start | bytes 208904 | tf_op jit(solution)/shard_map/ppermute | solution.py:586
  34.1 16.1 %collective-permute-start.1 = (f32[264,128]{1,0:T(8,128)S(1)}, f32[264,128]{1,0:T(8,128)S(1)}, u32[]{:S(2)}, u32[]{:S(2)}) collective-permute-start(f32[264,128]{1,0:T(8,128)S(1)} %get-tuple-element.32), channel_id=1, source_target_pairs={{0,64},{4,68},{8,72},{12,76},{16,80},{20,84},{24,88},{28,92},{32,9... | collective-permute-start | bytes 405512 | tf_op jit(solution)/shard_map/ppermute | solution.py:586
  35.4 14.8 %collective-permute-start.3 = (f32[264,128]{1,0:T(8,128)S(1)}, f32[264,128]{1,0:T(8,128)S(1)}, u32[]{:S(2)}, u32[]{:S(2)}) collective-permute-start(f32[264,128]{1,0:T(8,128)S(1)} %get-tuple-element.34), channel_id=1, source_target_pairs={{0,128},{4,132},{8,136},{12,140},{16,144},{20,148},{24,152},{28,15... | collective-permute-start | bytes 405512 | tf_op jit(solution)/shard_map/ppermute | solution.py:586
  36.8 13.4 %collective-permute-start.4 = (f32[264,128]{1,0:T(8,128)S(1)}, f32[264,128]{1,0:T(8,128)S(1)}, u32[]{:S(2)}, u32[]{:S(2)}) collective-permute-start(f32[264,128]{1,0:T(8,128)S(1)} %get-tuple-element.35), channel_id=1, source_target_pairs={{0,132},{4,128},{8,140},{12,136},{16,148},{20,144},{24,156},{28,15... | collective-permute-start | bytes 405512 | tf_op jit(solution)/shard_map/ppermute | solution.py:586
  38.1 12.1 %collective-permute-start.5 = (f32[264,128]{1,0:T(8,128)S(1)}, f32[264,128]{1,0:T(8,128)S(1)}, u32[]{:S(2)}, u32[]{:S(2)}) collective-permute-start(f32[264,128]{1,0:T(8,128)S(1)} %get-tuple-element.36), channel_id=1, source_target_pairs={{0,192},{4,196},{8,200},{12,204},{16,208},{20,212},{24,216},{28,22... | collective-permute-start | bytes 405512 | tf_op jit(solution)/shard_map/ppermute | solution.py:586
  39.8 10.4 %collective-permute-start.6 = (f32[200,128]{1,0:T(8,128)S(1)}, f32[200,128]{1,0:T(8,128)S(1)}, u32[]{:S(2)}, u32[]{:S(2)}) collective-permute-start(f32[200,128]{1,0:T(8,128)S(1)} %get-tuple-element.37), channel_id=1, source_target_pairs={{0,196},{4,192},{8,204},{12,200},{16,212},{20,208},{24,220},{28,21... | collective-permute-start | bytes 307208 | tf_op jit(solution)/shard_map/ppermute | solution.py:586
  51.8 17.4 %collective-permute-start.7 = (f32[272,128]{1,0:T(8,128)S(1)}, f32[272,128]{1,0:T(8,128)S(1)}, u32[]{:S(2)}, u32[]{:S(2)}) collective-permute-start(f32[272,128]{1,0:T(8,128)S(1)} %get-tuple-element.39), channel_id=1, source_target_pairs={{0,8},{4,12},{8,16},{12,20},{16,24},{20,28},{24,32},{28,36},{32,40... | collective-permute-start | bytes 417800 | tf_op jit(solution)/shard_map/ppermute | solution.py:586
  53.8 19.6 %collective-permute-start.8 = (f32[272,128]{1,0:T(8,128)S(1)}, f32[272,128]{1,0:T(8,128)S(1)}, u32[]{:S(2)}, u32[]{:S(2)}) collective-permute-start(f32[272,128]{1,0:T(8,128)S(1)} %get-tuple-element.40), channel_id=1, source_target_pairs={{0,56},{4,60},{8,0},{12,4},{16,8},{20,12},{24,16},{28,20},{32,24},... | collective-permute-start | bytes 417800 | tf_op jit(solution)/shard_map/ppermute | solution.py:586
  63.4 20.5 %collective-permute-start.12 = (f32[2,328,128]{2,1,0:T(8,128)S(1)}, f32[2,328,128]{2,1,0:T(8,128)S(1)}, u32[]{:S(2)}, u32[]{:S(2)}) collective-permute-start(f32[2,328,128]{2,1,0:T(8,128)S(1)} %get-tuple-element.47.rest_7_), channel_id=1, source_target_pairs={{0,1},{1,2},{2,3},{3,0},{4,5},{5,6},{6,7},{7,4},{8,9},{9,10},{10,1... | collective-permute-start | bytes 1007624 | tf_op jit(solution)/shard_map/ppermute | solution.py:595
  65.0 18.9 %collective-permute-start.13 = (f32[2,328,128]{2,1,0:T(8,128)S(1)}, f32[2,328,128]{2,1,0:T(8,128)S(1)}, u32[]{:S(2)}, u32[]{:S(2)}) collective-permute-start(f32[2,328,128]{2,1,0:T(8,128)S(1)} %get-tuple-element.48.rest_8_), channel_id=1, source_target_pairs={{0,2},{1,3},{2,0},{3,1},{4,6},{5,7},{6,4},{7,5},{8,10},{9,11},{10,... | collective-permute-start | bytes 1007624 | tf_op jit(solution)/shard_map/ppermute | solution.py:595
  67.7 16.2 %collective-permute-start.14 = (f32[2,328,128]{2,1,0:T(8,128)S(1)}, f32[2,328,128]{2,1,0:T(8,128)S(1)}, u32[]{:S(2)}, u32[]{:S(2)}) collective-permute-start(f32[2,328,128]{2,1,0:T(8,128)S(1)} %get-tuple-element.49.rest_9_), channel_id=1, source_target_pairs={{0,3},{1,0},{2,1},{3,2},{4,7},{5,4},{6,5},{7,6},{8,11},{9,8},{10,9... | collective-permute-start | bytes 1007624 | tf_op jit(solution)/shard_map/ppermute | solution.py:595
  69.2 9.8 %collective-permute-start.9 = (f32[136,128]{1,0:T(8,128)S(1)}, f32[136,128]{1,0:T(8,128)S(1)}, u32[]{:S(2)}, u32[]{:S(2)}) collective-permute-start(f32[136,128]{1,0:T(8,128)S(1)} %get-tuple-element.41), channel_id=1, source_target_pairs={{0,32},{4,36},{8,40},{12,44},{16,48},{20,52},{24,56},{28,60},{32,0... | collective-permute-start | bytes 208904 | tf_op jit(solution)/shard_map/ppermute | solution.py:586
  73.4 10.5 %collective-permute-start.10 = (f32[136,128]{1,0:T(8,128)S(1)}, f32[136,128]{1,0:T(8,128)S(1)}, u32[]{:S(2)}, u32[]{:S(2)}) collective-permute-start(f32[136,128]{1,0:T(8,128)S(1)} %get-tuple-element.44), channel_id=1, source_target_pairs={{0,16},{4,20},{8,24},{12,28},{16,32},{20,36},{24,40},{28,44},{32,4... | collective-permute-start | bytes 208904 | tf_op jit(solution)/shard_map/ppermute | solution.py:586
  79.0 5.2 %collective-permute-start.11 = (f32[136,128]{1,0:T(8,128)S(1)}, f32[136,128]{1,0:T(8,128)S(1)}, u32[]{:S(2)}, u32[]{:S(2)}) collective-permute-start(f32[136,128]{1,0:T(8,128)S(1)} %get-tuple-element.45), channel_id=1, source_target_pairs={{0,48},{4,52},{8,56},{12,60},{16,0},{20,4},{24,8},{28,12},{32,16},... | collective-permute-start | bytes 208904 | tf_op jit(solution)/shard_map/ppermute | solution.py:586
